TPU v7x, 128 devices: a whole 4x4x4 slice. The times are simulated.
128 devices in a mesh: tm: 8 (over y, core), height: 16 (over z, x).
Axes of the slice: x: 4, y: 4, z: 4, core: 2. Of those that a mesh axis runs over, the one named last changes fastest.
Arguments:
- queries: bfloat16 [8, 16, 2, 64, 3072], P('tm', 'height'), may hold values from -40 to 40
- keys_values: bfloat16 [8, 16, 2, 2, 64, 3072], P('tm', 'height'), may hold values from -6.2 to 6.2
- far_cubes: int32 [8, 16, 2, 24, 16], P('tm', 'height'), may hold values from 0 to 255, as said below
- out_weight: bfloat16 [3072, 3072], replicated, may hold values from -0.59765625 to 0.59765625
Outputs:
- output: bfloat16 [8, 16, 2, 64, 3072], P('tm', 'height')
Inputs may be any that keep to these rules, and one draw needn't show every extreme that they name: `far_cubes`: the 16 cubes of one list are distinct. Over all cubes that one device holds, the distinct pairs (far cube, head) whose cube lies on one given device number at most 4, and exactly 4 for some given devices, from every device.
All inputs are finite; a program needn't handle non-finite values.
Results may differ from a plain program's by a relative error of at most 0.0058.
Values may be sent and summed in bfloat16 or wider, within the bound.
A program may use at most 256 MiB of HBM per device.

v0:
```python
import math

import jax
import jax.numpy as jnp
from jax import lax
from jax.sharding import PartitionSpec as P

HEADS = 24
SLOTS = 512


def padded_2(shard, sides, width):
    for axis, dim in sides:
        peers, length = (lax.axis_size(axis), shard.shape[dim])
        up = [(i, (i + 1) % peers) for i in range(peers - 1)]
        down = [(j, i) for i, j in up]
        last = lax.slice_in_dim(shard, length - width, length, axis=dim)
        leading = lax.slice_in_dim(shard, 0, width, axis=dim)
        before = lax.ppermute(last, axis, up)
        after = lax.ppermute(leading, axis, down)
        shard = jnp.concatenate([before, shard, after], axis=dim)
    return shard


def body(queries, keys_values, far_cubes, out_weight):
    tm_count = lax.axis_size("tm")
    height_count = lax.axis_size("height")
    device_count = tm_count * height_count
    capacity = SLOTS // device_count
    span_time, span_height, span_width, cube, width = queries.shape
    heads = HEADS
    head_size = width // heads
    far_count = far_cubes.shape[-1]
    local_count = span_time * span_height * span_width
    grid_time = span_time * tm_count
    grid_height = span_height * height_count
    far_ids = far_cubes.reshape(local_count, heads, far_count)
    far_time = far_ids // (grid_height * span_width)
    far_height = far_ids // span_width % grid_height
    far_width = far_ids % span_width
    owner_dev = far_time // span_time * height_count + far_height // span_height
    local_cube = (
        far_time % span_time * span_height + far_height % span_height
    ) * span_width + far_width
    tile_code = local_cube * heads + jnp.arange(heads, dtype=jnp.int32)[None, :, None]
    wanted = (
        jnp.zeros((device_count, local_count * heads), jnp.int32).at[owner_dev, tile_code].max(1)
    )
    slot_rank = jnp.cumsum(wanted, axis=1) - 1
    far_slot = owner_dev * capacity + slot_rank[owner_dev, tile_code]
    target = jnp.where(wanted > 0, slot_rank, capacity)
    columns = jnp.broadcast_to(
        jnp.arange(local_count * heads, dtype=jnp.int32)[None, :], wanted.shape
    )
    rows = jnp.broadcast_to(jnp.arange(device_count, dtype=jnp.int32)[:, None], wanted.shape)
    requests = (
        jnp.zeros((device_count, capacity + 1), jnp.int32)
        .at[rows, target]
        .set(columns)[:, :capacity]
    )
    source = keys_values.reshape(local_count, 2, cube, heads, head_size)
    padded = padded_2(keys_values, (("tm", 0), ("height", 1)), 1)
    padded = jnp.pad(padded, ((0, 0), (0, 0), (1, 1), (0, 0), (0, 0), (0, 0)))
    asked = lax.all_to_all(requests, ("tm", "height"), split_axis=0, concat_axis=0, tiled=True)
    tiles = lax.all_to_all(
        source[asked // heads, :, :, asked % heads, :],
        ("tm", "height"),
        split_axis=0,
        concat_axis=0,
        tiled=True,
    )
    received = tiles.reshape(device_count * capacity, 2, cube, head_size)
    first_time = lax.axis_index("tm") * span_time
    first_height = lax.axis_index("height") * span_height
    offsets = jnp.arange(3, dtype=jnp.int32) - 1
    scale = 1.0 / math.sqrt(head_size)
    zero = jnp.zeros((), jnp.int32)
    flat_queries = queries.reshape(local_count, cube, heads, head_size)

    def one_cube(index):
        time_pos = index // (span_height * span_width)
        height_pos = index // span_width % span_height
        width_pos = index % span_width
        window = lax.dynamic_slice(
            padded, (time_pos, height_pos, width_pos, zero, zero, zero), (3, 3, 3, 2, cube, width)
        )
        window = window.reshape(27, 2, cube, heads, head_size)
        global_time = first_time + time_pos + offsets
        global_height = first_height + height_pos + offsets
        global_width = width_pos + offsets
        inside_time = (global_time >= 0) & (global_time < grid_time)
        inside_height = (global_height >= 0) & (global_height < grid_height)
        inside_width = (global_width >= 0) & (global_width < span_width)
        valid = (
            inside_time[:, None, None] & inside_height[None, :, None] & inside_width[None, None, :]
        ).reshape(27)
        keys_window = window[:, 0].reshape(27 * cube, heads, head_size)
        values_window = window[:, 1].reshape(27 * cube, heads, head_size)
        far_tiles = received[far_slot[index]]
        query = flat_queries[index]
        score_window = (
            jnp.einsum("qhd,khd->hqk", query, keys_window, preferred_element_type=jnp.float32)
            * scale
        )
        score_window = jnp.where(jnp.repeat(valid, cube)[None, None, :], score_window, -jnp.inf)
        score_far = (
            jnp.einsum(
                "qhd,hfkd->hqfk", query, far_tiles[:, :, 0], preferred_element_type=jnp.float32
            )
            * scale
        )
        scores = jnp.concatenate(
            [score_window, score_far.reshape(heads, cube, far_count * cube)], axis=-1
        )
        largest = jnp.max(scores, axis=-1, keepdims=True)
        lifted = jnp.exp(scores - largest)
        weights = (lifted / jnp.sum(lifted, axis=-1, keepdims=True)).astype(jnp.bfloat16)
        attended = jnp.einsum(
            "hqk,khd->qhd",
            weights[:, :, : 27 * cube],
            values_window,
            preferred_element_type=jnp.float32,
        )
        far_weights = weights[:, :, 27 * cube :].reshape(heads, cube, far_count, cube)
        attended = attended + jnp.einsum(
            "hqfk,hfkd->qhd", far_weights, far_tiles[:, :, 1], preferred_element_type=jnp.float32
        )
        return attended.reshape(cube, width).astype(jnp.bfloat16)

    attended = lax.map(one_cube, jnp.arange(local_count, dtype=jnp.int32))
    output = jnp.dot(
        attended.reshape(local_count * cube, width), out_weight, preferred_element_type=jnp.float32
    )
    return output.astype(jnp.bfloat16).reshape(queries.shape)


def solution(mesh):
    in_specs = (
        P("tm", "height", None, None, None),
        P("tm", "height", None, None, None, None),
        P("tm", "height", None, None, None),
        P(),
    )
    out_specs = P("tm", "height", None, None, None)
    return jax.shard_map(body, mesh=mesh, in_specs=in_specs, out_specs=out_specs, check_vma=False)
```

profile of v0, /device:TPU:1, one launch (start us, length us, event | category | flops | bytes accessed | tf_op | source)
XLA Modules:
  0.0 757.9 jit_solution(3496498932481911336)
XLA Ops:
  1.0 36.7 %scatter_fusion = s32[128,48]{0,1:T(8,128)S(1)} fusion(s32[128,48]{0,1:T(8,128)S(1)} %broadcast.592, s32[768]{0:T(1024)S(1)} %reshape.498, s32[768]{0:T(1024)S(1)} %broadcast.656), kind=kCustom, calls=%fused_computation.3 | custom fusion | flops 768 | bytes 15360 | tf_op jit(solution)/shard_map/scatter-max | solution.py:47
  38.3 23.0 %scatter_custom_fusion.1 = s32[640]{0:T(1024)S(1)} fusion(s32[6144]{0:T(1024)S(1)} %reshape.504, s32[6144]{0:T(1024)S(1)} %reshape.506, s32[]{:T(128)} %constant.230.clone.1), kind=kCustom, calls=%fused_computation.124 | custom fusion | bytes 2564
  62.0 11.5 %all-to-all-start = ((s32[128,1,4]{2,1,0:T(1,128)}), s32[128,1,4]{2,1,0:T(1,128)S(1)}, u32[]{:S(2)}, u32[]{:S(2)}) async-start(s32[128,1,4]{2,1,0:T(1,128)} %copy.50), calls=%async_computation | async-start | bytes 131072 | tf_op jit(solution)/shard_map/all_to_all | solution.py:64
  74.2 9.0 %all-to-all-done = s32[128,1,4]{2,1,0:T(1,128)S(1)} async-done(((s32[128,1,4]{2,1,0:T(1,128)}), s32[128,1,4]{2,1,0:T(1,128)S(1)}, u32[]{:S(2)}, u32[]{:S(2)}) %all-to-all-start) | async-done | bytes 2080 | tf_op jit(solution)/shard_map/all_to_all | solution.py:64
  83.5 10.9 %gather_fusion.2 = bf16[512,2,64,128]{3,2,1,0:T(8,128)(2,1)} fusion(bf16[2,2,64,24,128]{4,2,3,1,0:T(8,128)(2,1)S(1)} %copy.55, s32[512]{0:T(512)S(1)} %reshape.492), kind=kCustom, calls=%fused_computation.2 | custom fusion | bytes 33558528 | tf_op jit(solution)/shard_map/gather | solution.py:66
  105.6 224.3 %collective-permute-done = bf16[1,1,2,2,64,3072]{5,4,3,2,1,0:T(8,128)(2,1)S(1)} collective-permute-done((bf16[1,1,2,2,64,3072]{5,4,3,2,1,0:T(8,128)(2,1)S(1)}, bf16[1,1,2,2,64,3072]{5,4,3,2,1,0:T(8,128)(2,1)S(1)}, u32[]{:S(2)}, u32[]{:S(2)}) %collective-permute-start) | collective-permute-done | bytes 1572896 | tf_op jit(solution)/shard_map/ppermute | solution.py:19
  332.5 17.2 %collective-permute-done.1 = bf16[1,1,2,2,64,3072]{5,4,3,2,1,0:T(8,128)(2,1)S(1)} collective-permute-done((bf16[1,1,2,2,64,3072]{5,4,3,2,1,0:T(8,128)(2,1)S(1)}, bf16[1,1,2,2,64,3072]{5,4,3,2,1,0:T(8,128)(2,1)S(1)}, u32[]{:S(2)}, u32[]{:S(2)}) %collective-permute-start.1) | collective-permute-done | bytes 1572896 | tf_op jit(solution)/shard_map/ppermute | solution.py:20
  362.2 44.0 %collective-permute-done.2 = bf16[3,1,2,2,64,3072]{5,4,3,2,1,0:T(8,128)(2,1)} collective-permute-done((bf16[3,1,2,2,64,3072]{5,4,3,2,1,0:T(8,128)(2,1)}, bf16[3,1,2,2,64,3072]{5,4,3,2,1,0:T(8,128)(2,1)}, u32[]{:S(2)}, u32[]{:S(2)}) %collective-permute-start.2) | collective-permute-done | bytes 4718624 | tf_op jit(solution)/shard_map/ppermute | solution.py:19
  406.1 31.0 %collective-permute-done.3 = bf16[3,1,2,2,64,3072]{5,4,3,2,1,0:T(8,128)(2,1)} collective-permute-done((bf16[3,1,2,2,64,3072]{5,4,3,2,1,0:T(8,128)(2,1)}, bf16[3,1,2,2,64,3072]{5,4,3,2,1,0:T(8,128)(2,1)}, u32[]{:S(2)}, u32[]{:S(2)}) %collective-permute-start.3) | collective-permute-done | bytes 4718624 | tf_op jit(solution)/shard_map/ppermute | solution.py:20
  437.2 13.6 %fusion.33 = bf16[3,3,4,2,64,3072]{5,4,3,2,1,0:T(8,128)(2,1)} fusion(bf16[3,1,2,2,64,3072]{5,4,3,2,1,0:T(8,128)(2,1)} %collective-permute-done.3, bf16[3,1,2,2,64,3072]{5,4,3,2,1,0:T(8,128)(2,1)} %constant_dynamic-update-slice_fusion.1, bf16[3,1,2,2,64,3072]{5,4,3,2,1,0:T(8,128)(2,1)} %collective-permute-done.2), kind=kLoop, calls=%fused_computation.48 | loop fusion | flops 169869312 | bytes 42467328 | tf_op jit(solution)/shard_map/concatenate | solution.py:21
  450.8 297.0 %while.14 = (s32[]{:T(128)}, bf16[2,64,3072]{2,1,0:T(8,128)(2,1)}, s32[2]{0:T(128)S(1)}, bf16[3,3,4,2,64,3072]{5,4,3,2,1,0:T(8,128)(2,1)}, s32[]{:T(128)}, /*ind...) while((s32[]{:T(128)}, bf16[2,64,3072]{2,1,0:T(8,128)(2,1)}, ...), condition=%wide.region_7.8_spmd.clone.clone, body=%wide.region_3.7_spmd.clone.clone.sunk | while | flops 2205351168 | bytes 497691072 | solution.py:130
  453.5 15.1 %constant_dynamic-slice_fusion.5 = bf16[3,3,3,2,64,3072]{5,4,3,2,1,0:T(8,128)(2,1)} fusion(bf16[3,3,4,2,64,3072]{5,4,3,2,1,0:T(8,128)(2,1)} %get-tuple-element.345, s32[]{:T(128)S(6)} %select_n.356), kind=kLoop, calls=%fused_computation.35.clone.1 | loop fusion | bytes 42467332 | tf_op jit(solution)/shard_map/while/body/eval_jaxpr/dynamic_slice | solution.py:84
  468.7 12.1 %copy.94 = bf16[432,8,24,128]{3,2,1,0:T(8,128)(2,1)S(1)} copy(bf16[432,8,24,128]{3,1,2,0:T(8,128)(2,1)} %bitcast.180) | data formatting | bytes 42467328 | tf_op jit(solution)/shard_map/while
  480.8 7.0 fusion.89
  497.5 11.7 %fusion.90 = (f32[24,64]{1,0:T(8,128)S(1)}, f32[24,64,1728]{2,1,0:T(8,128)}) fusion(bf16[1728,24,128]{2,0,1:T(8,128)(2,1)} %bitcast.184, bf16[1,64,24,128]{3,2,1,0:T(8,128)(2,1)S(1)} %constant_dynamic-slice_fusion.4, pred[1728]{0:T(1024)(128)(4,1)S(1)} %broadcast_in_dim.91), kind=kOutput, calls=%fused_computation.132.clone.1 | convolution fusion | flops 687438336 | bytes 21634752 | tf_op jit(solution)/shard_map/while/body/eval_jaxpr/qhd,khd->hqk/dot_general | solution.py:102
  509.3 17.1 %gather_fusion = bf16[384,2,64,128]{3,2,1,0:T(8,128)(2,1)} fusion(bf16[512,2,64,128]{3,2,1,0:T(8,128)(2,1)} %get-tuple-element.350, s32[1024]{0:T(1024)S(1)} %pad_clamp_fusion.2), kind=kCustom, calls=%fused_computation.clone.clone.1 | custom fusion | bytes 25167360 | tf_op jit(solution)/shard_map/while/body/eval_jaxpr/gather | solution.py:99
  542.7 9.7 %copy.93 = f32[24,64,1024]{2,1,0:T(8,128)} copy(f32[24,64,1024]{1,2,0:T(8,128)} %bitcast.183) | data formatting | bytes 12582912 | tf_op jit(solution)/shard_map/while/body/eval_jaxpr/reshape | solution.py:113
  552.4 9.1 %fusion.91 = f32[24,64]{1,0:T(8,128)S(1)} fusion(f32[24,64,1024]{2,1,0:T(8,128)} %copy.93, f32[24,64,1728]{2,1,0:T(8,128)} %get-tuple-element.310, f32[24,64]{1,0:T(8,128)S(1)} %reduce_max.36), kind=kLoop, calls=%fused_computation.9.clone.1 | loop fusion | flops 12679680 | bytes 16920576 | tf_op jit(solution)/shard_map/while/body/eval_jaxpr/reduce_sum | solution.py:117
  561.6 7.9 %divide_convert_fusion.2 = bf16[24,64,2752]{2,1,0:T(8,128)(2,1)S(1)} fusion(f32[24,64,1024]{2,1,0:T(8,128)S(1)} %copy-done, f32[24,64,1728]{2,1,0:T(8,128)} %get-tuple-element.310, f32[24,64]{1,0:T(8,128)S(1)} %fusion.91, f32[24,64]{1,0:T(8,128)S(1)} %reduce_max.36), kind=kLoop, calls=%fused_computation.8.clone.1 | loop fusion | flops 16908288 | bytes 25374720 | tf_op jit(solution)/shard_map/while/body/eval_jaxpr/convert_element_type | solution.py:117
  580.7 7.3 fusion.92
  588.1 7.6 copy.96
  601.9 15.1 %constant_dynamic-slice_fusion.5 = bf16[3,3,3,2,64,3072]{5,4,3,2,1,0:T(8,128)(2,1)} fusion(bf16[3,3,4,2,64,3072]{5,4,3,2,1,0:T(8,128)(2,1)} %get-tuple-element.345, s32[]{:T(128)S(6)} %select_n.356), kind=kLoop, calls=%fused_computation.35.clone.1 | loop fusion | bytes 42467332 | tf_op jit(solution)/shard_map/while/body/eval_jaxpr/dynamic_slice | solution.py:84
  617.0 12.1 %copy.94 = bf16[432,8,24,128]{3,2,1,0:T(8,128)(2,1)S(1)} copy(bf16[432,8,24,128]{3,1,2,0:T(8,128)(2,1)} %bitcast.180) | data formatting | bytes 42467328 | tf_op jit(solution)/shard_map/while
  629.1 7.0 fusion.89
  645.9 11.7 %fusion.90 = (f32[24,64]{1,0:T(8,128)S(1)}, f32[24,64,1728]{2,1,0:T(8,128)}) fusion(bf16[1728,24,128]{2,0,1:T(8,128)(2,1)} %bitcast.184, bf16[1,64,24,128]{3,2,1,0:T(8,128)(2,1)S(1)} %constant_dynamic-slice_fusion.4, pred[1728]{0:T(1024)(128)(4,1)S(1)} %broadcast_in_dim.91), kind=kOutput, calls=%fused_computation.132.clone.1 | convolution fusion | flops 687438336 | bytes 21634752 | tf_op jit(solution)/shard_map/while/body/eval_jaxpr/qhd,khd->hqk/dot_general | solution.py:102
  657.7 17.1 %gather_fusion = bf16[384,2,64,128]{3,2,1,0:T(8,128)(2,1)} fusion(bf16[512,2,64,128]{3,2,1,0:T(8,128)(2,1)} %get-tuple-element.350, s32[1024]{0:T(1024)S(1)} %pad_clamp_fusion.2), kind=kCustom, calls=%fused_computation.clone.clone.1 | custom fusion | bytes 25167360 | tf_op jit(solution)/shard_map/while/body/eval_jaxpr/gather | solution.py:99
  691.1 9.7 %copy.93 = f32[24,64,1024]{2,1,0:T(8,128)} copy(f32[24,64,1024]{1,2,0:T(8,128)} %bitcast.183) | data formatting | bytes 12582912 | tf_op jit(solution)/shard_map/while/body/eval_jaxpr/reshape | solution.py:113
  700.8 9.1 %fusion.91 = f32[24,64]{1,0:T(8,128)S(1)} fusion(f32[24,64,1024]{2,1,0:T(8,128)} %copy.93, f32[24,64,1728]{2,1,0:T(8,128)} %get-tuple-element.310, f32[24,64]{1,0:T(8,128)S(1)} %reduce_max.36), kind=kLoop, calls=%fused_computation.9.clone.1 | loop fusion | flops 12679680 | bytes 16920576 | tf_op jit(solution)/shard_map/while/body/eval_jaxpr/reduce_sum | solution.py:117
  710.0 7.9 %divide_convert_fusion.2 = bf16[24,64,2752]{2,1,0:T(8,128)(2,1)S(1)} fusion(f32[24,64,1024]{2,1,0:T(8,128)S(1)} %copy-done, f32[24,64,1728]{2,1,0:T(8,128)} %get-tuple-element.310, f32[24,64]{1,0:T(8,128)S(1)} %fusion.91, f32[24,64]{1,0:T(8,128)S(1)} %reduce_max.36), kind=kLoop, calls=%fused_computation.8.clone.1 | loop fusion | flops 16908288 | bytes 25374720 | tf_op jit(solution)/shard_map/while/body/eval_jaxpr/convert_element_type | solution.py:117
  729.1 7.3 fusion.92
  736.5 7.6 copy.96
  747.7 10.1 %convolution_convert_fusion = bf16[128,3072]{1,0:T(8,128)(2,1)} fusion(bf16[128,3072]{1,0:T(8,128)(2,1)} %bitcast.190, bf16[3072,3072]{1,0:T(8,128)(2,1)} %param.9), kind=kOutput, calls=%fused_computation.49 | convolution fusion | flops 2416312320 | bytes 20447232 | tf_op jit(solution)/shard_map/dot_general | solution.py:131
  (129 shorter events, 108.5 us)
Async XLA Ops:
  0.9 36.9 %copy-start.9 = (s32[2]{0:T(128)S(1)}, s32[2]{0:T(128)}, u32[]{:S(2)}) copy-start(s32[2]{0:T(128)} %constant.251) | copy-start | bytes 28
  0.9 36.9 %copy-start.8 = (s32[2]{0:T(128)S(1)}, s32[2]{0:T(128)}, u32[]{:S(2)}) copy-start(s32[2]{0:T(128)} %constant.254) | copy-start | bytes 28
  1.0 72.6 %copy-start.3 = (bf16[1,1,2,2,64,3072]{5,4,3,2,1,0:T(8,128)(2,1)S(1)}, bf16[1,1,2,2,64,3072]{5,4,3,2,1,0:T(8,128)(2,1)}, u32[]{:S(2)}) copy-start(bf16[1,1,2,2,64,3072]{5,4,3,2,1,0:T(8,128)(2,1)} %param.7) | copy-start | bytes 4718596
  62.0 21.2 %all-to-all-start = ((s32[128,1,4]{2,1,0:T(1,128)}), s32[128,1,4]{2,1,0:T(1,128)S(1)}, u32[]{:S(2)}, u32[]{:S(2)}) async-start(s32[128,1,4]{2,1,0:T(1,128)} %copy.50), calls=%async_computation | async-start | bytes 131072 | tf_op jit(solution)/shard_map/all_to_all | solution.py:64
  94.4 261.2 %copy-start.7 = (s32[1,1,2,24,16]{3,4,2,1,0:T(8,128)S(1)}, s32[1,1,2,24,16]{3,4,2,1,0:T(8,128)}, u32[]{:S(2)}) copy-start(s32[1,1,2,24,16]{3,4,2,1,0:T(8,128)} %param.8) | copy-start | bytes 9220
  94.4 356.3 %all-to-all-start.1 = ((bf16[128,4,2,64,128]{4,3,2,1,0:T(8,128)(2,1)}), bf16[128,4,2,64,128]{4,3,2,1,0:T(8,128)(2,1)}, u32[]{:S(2)}, u32[]{:S(2)}) async-start(bf16[128,4,2,64,128]{4,3,2,1,0:T(8,128)(2,1)} %bitcast.187), calls=%async_computation.1 | async-start | bytes 33554432 | tf_op jit(solution)/shard_map/all_to_all | solution.py:65
  100.1 229.9 %collective-permute-start = (bf16[1,1,2,2,64,3072]{5,4,3,2,1,0:T(8,128)(2,1)S(1)}, bf16[1,1,2,2,64,3072]{5,4,3,2,1,0:T(8,128)(2,1)S(1)}, u32[]{:S(2)}, u32[]{:S(2)}) collective-permute-start(bf16[1,1,2,2,64,3072]{5,4,3,2,1,0:T(8,128)(2,1)S(1)} %copy-done.3), channel_id=1, source_target_pairs={{0,16},{16,32},{32,48},{48,64},{64,80},{80,96},{96,112},{1,17},{17... | collective-permute-start | bytes 4718600 | tf_op jit(solution)/shard_map/ppermute | solution.py:19
  103.7 246.0 %collective-permute-start.1 = (bf16[1,1,2,2,64,3072]{5,4,3,2,1,0:T(8,128)(2,1)S(1)}, bf16[1,1,2,2,64,3072]{5,4,3,2,1,0:T(8,128)(2,1)S(1)}, u32[]{:S(2)}, u32[]{:S(2)}) collective-permute-start(bf16[1,1,2,2,64,3072]{5,4,3,2,1,0:T(8,128)(2,1)S(1)} %copy-done.3), channel_id=1, source_target_pairs={{16,0},{32,16},{48,32},{64,48},{80,64},{96,80},{112,96},{17,1},{33... | collective-permute-start | bytes 4718600 | tf_op jit(solution)/shard_map/ppermute | solution.py:20
  350.9 55.2 %collective-permute-start.2 = (bf16[3,1,2,2,64,3072]{5,4,3,2,1,0:T(8,128)(2,1)}, bf16[3,1,2,2,64,3072]{5,4,3,2,1,0:T(8,128)(2,1)}, u32[]{:S(2)}, u32[]{:S(2)}) collective-permute-start(bf16[3,1,2,2,64,3072]{5,4,3,2,1,0:T(8,128)(2,1)} %constant_dynamic-update-slice_fusion.1), channel_id=1, source_target_pairs={{0,1},{1,2},{2,3},{3,4},{4,5},{5,6},{6,7},{7,8},{8,9},{9,10},{10,1... | collective-permute-start | bytes 14155784 | tf_op jit(solution)/shard_map/ppermute | solution.py:19
  354.4 82.8 %collective-permute-start.3 = (bf16[3,1,2,2,64,3072]{5,4,3,2,1,0:T(8,128)(2,1)}, bf16[3,1,2,2,64,3072]{5,4,3,2,1,0:T(8,128)(2,1)}, u32[]{:S(2)}, u32[]{:S(2)}) collective-permute-start(bf16[3,1,2,2,64,3072]{5,4,3,2,1,0:T(8,128)(2,1)} %constant_dynamic-update-slice_fusion.1), channel_id=1, source_target_pairs={{1,0},{2,1},{3,2},{4,3},{5,4},{6,5},{7,6},{8,7},{9,8},{10,9},{11,1... | collective-permute-start | bytes 14155784 | tf_op jit(solution)/shard_map/ppermute | solution.py:20
  355.9 5.2 copy-start.6
  532.7 4.5 copy-start.2
  552.4 9.2 %copy-start = (f32[24,64,1024]{2,1,0:T(8,128)S(1)}, f32[24,64,1024]{2,1,0:T(8,128)}, u32[]{:S(2)}) copy-start(f32[24,64,1024]{2,1,0:T(8,128)} %copy.93) | copy-start | bytes 18874372 | tf_op jit(solution)/shard_map/while
  569.5 3.4 copy-start.1
  588.1 7.6 %slice-start = ((s8[8650752]{0:T(1024)(128)(4,1)}), s8[4194304]{0:T(1024)(128)(4,1)S(1)}, s32[]{:S(2)}) async-start(s8[8650752]{0:T(1024)(128)(4,1)} %bitcast.181), calls=%async_computation.2 | async-start | bytes 8388608 | tf_op jit(solution)/shard_map/while
  588.1 7.6 %slice-start.1 = ((s8[8650752]{0:T(1024)(128)(4,1)}), s8[4194304]{0:T(1024)(128)(4,1)S(1)}, s32[]{:S(2)}) async-start(s8[8650752]{0:T(1024)(128)(4,1)} %bitcast.181), calls=%async_computation.3 | async-start | bytes 8388608 | tf_op jit(solution)/shard_map/while
  588.1 7.6 %slice-start.2 = ((s8[8650752]{0:T(1024)(128)(4,1)}), s8[262144]{0:T(1024)(128)(4,1)S(1)}, s32[]{:S(2)}) async-start(s8[8650752]{0:T(1024)(128)(4,1)} %bitcast.181), calls=%async_computation.4 | async-start | bytes 524288 | tf_op jit(solution)/shard_map/while
  595.7 2.7 copy-start.4
  598.5 0.9 copy-start.5
  681.0 4.5 copy-start.2
  700.8 9.2 %copy-start = (f32[24,64,1024]{2,1,0:T(8,128)S(1)}, f32[24,64,1024]{2,1,0:T(8,128)}, u32[]{:S(2)}) copy-start(f32[24,64,1024]{2,1,0:T(8,128)} %copy.93) | copy-start | bytes 18874372 | tf_op jit(solution)/shard_map/while
  717.9 3.4 copy-start.1
  736.4 7.6 %slice-start = ((s8[8650752]{0:T(1024)(128)(4,1)}), s8[4194304]{0:T(1024)(128)(4,1)S(1)}, s32[]{:S(2)}) async-start(s8[8650752]{0:T(1024)(128)(4,1)} %bitcast.181), calls=%async_computation.2 | async-start | bytes 8388608 | tf_op jit(solution)/shard_map/while
  736.5 7.6 %slice-start.1 = ((s8[8650752]{0:T(1024)(128)(4,1)}), s8[4194304]{0:T(1024)(128)(4,1)S(1)}, s32[]{:S(2)}) async-start(s8[8650752]{0:T(1024)(128)(4,1)} %bitcast.181), calls=%async_computation.3 | async-start | bytes 8388608 | tf_op jit(solution)/shard_map/while
  736.5 7.6 %slice-start.2 = ((s8[8650752]{0:T(1024)(128)(4,1)}), s8[262144]{0:T(1024)(128)(4,1)S(1)}, s32[]{:S(2)}) async-start(s8[8650752]{0:T(1024)(128)(4,1)} %bitcast.181), calls=%async_computation.4 | async-start | bytes 524288 | tf_op jit(solution)/shard_map/while
  744.1 2.7 copy-start.4
  746.9 0.9 copy-start.5
where the time goes:
time: 767 us; the launch traced here: 758 us
  waiting for transfers between devices  325 us (42%)
  local copies, waits for them, and re-layouts  247 us (32%)
  other arithmetic  85.9 us (11%)
  matrix products  63.6 us (8%)
  starting transfers between devices  27.4 us (4%)
  loops' own time  8.33 us (1%)
    ppermute x2, waiting for transfers between devices, padded_2(): before = lax.ppermute(last, axis, up)  268 us
    ppermute x2, waiting for transfers between devices, padded_2(): after = lax.ppermute(leading, axis, down)  48.2 us
    gather x4, local copies, waits for them, and re-layouts, one_cube(): far_tiles = received[far_slot[index]]  46.8 us
    while x34, local copies, waits for them, and re-layouts  41.9 us
    another operation x1, other arithmetic, body(): jnp.zeros((device_count, local_count * heads), jnp.int32)  36.7 us
    dynamic_slice x2, local copies, waits for them, and re-layouts, one_cube(): lax.dynamic_slice(padded, (time_pos, height_pos, width_pos, zero, zero, z...  30.3 us
    slice x4, local copies, waits for them, and re-layouts, one_cube(): values_window = window[:, 1].reshape(27 * cube, heads, head_size)  29.2 us
    unnamed x18, local copies, waits for them, and re-layouts  27.1 us
  transfers between devices with their start and end apart: 6, of which 5 were waited for; matrix products, arithmetic and copies ran while one was open for 3% of the time, Pallas kernels for 0%

commit v1 on v0

v1 whole, which is shorter than its diff:
```python
import functools
import math

import jax
import jax.numpy as jnp
from jax import lax
from jax.experimental import pallas as pl
from jax.experimental.pallas import tpu as pltpu
from jax.sharding import PartitionSpec as P

HEADS = 24
HEAD_DIM = 128
CUBE = 64
FAR = 16
NW = 2
SLOTS = 512
PAIR = 2
ROWS = NW * CUBE
NEG = -1e30
EXP2_SCALE = math.log2(math.e) / math.sqrt(HEAD_DIM)


def request_tables(far, device_count):
    capacity = SLOTS // device_count
    cubes = device_count * NW
    hit = far[:, :, :, None] == jnp.arange(cubes, dtype=jnp.int32)
    wanted = jnp.any(hit, axis=(0, 2))
    wanted = jnp.transpose(wanted.reshape(HEADS, device_count, NW), (1, 2, 0))
    wanted = wanted.reshape(device_count, NW * HEADS)
    codes = jnp.arange(NW * HEADS, dtype=jnp.int32)
    before = (codes[:, None] < codes[None, :]).astype(jnp.bfloat16)
    rank = jnp.dot(wanted.astype(jnp.bfloat16), before, preferred_element_type=jnp.float32)
    rank = rank.astype(jnp.int32)
    chosen = wanted[:, :, None] & (rank[:, :, None] == jnp.arange(capacity, dtype=jnp.int32))
    requests = jnp.sum(jnp.where(chosen, codes[None, :, None], 0), axis=1)
    slot = rank + jnp.arange(device_count, dtype=jnp.int32)[:, None] * capacity
    slot = jnp.transpose(slot.reshape(device_count, NW, HEADS), (2, 0, 1)).reshape(HEADS, cubes)
    far_slot = jnp.sum(jnp.where(hit, slot[None, :, None, :], 0), axis=-1)
    return requests, far_slot


def gather_kernel(asked_ref, kv_ref, out_ref, sem):
    def start(i, carry):
        code = asked_ref[i]
        lane = pl.multiple_of(code % HEADS * HEAD_DIM, HEAD_DIM)
        pltpu.make_async_copy(
            kv_ref.at[code // HEADS, :, :, pl.ds(lane, HEAD_DIM)], out_ref.at[i], sem
        ).start()
        return carry

    lax.fori_loop(0, SLOTS, start, 0)
    pltpu.make_async_copy(out_ref, out_ref, sem).wait()


def gather_tiles(asked, kv):
    return pl.pallas_call(
        gather_kernel,
        name="gather_tiles",
        out_shape=jax.ShapeDtypeStruct((SLOTS, 2, CUBE, HEAD_DIM), kv.dtype),
        grid_spec=pltpu.PrefetchScalarGridSpec(
            num_scalar_prefetch=1,
            grid=(1,),
            in_specs=[pl.BlockSpec(kv.shape, lambda i, a: (0, 0, 0, 0))],
            out_specs=pl.BlockSpec(memory_space=pl.ANY),
            scratch_shapes=[pltpu.SemaphoreType.DMA],
        ),
        cost_estimate=pl.CostEstimate(
            flops=0, bytes_accessed=2 * SLOTS * 2 * CUBE * HEAD_DIM, transcendentals=0
        ),
    )(asked, kv)


def window_kernel(valid_ref, q_ref, *refs):
    blocks, (acc_ref, stat_ref) = refs[:9], refs[9:]
    for p in range(PAIR):
        lanes = slice(p * HEAD_DIM, (p + 1) * HEAD_DIM)
        query = q_ref[:, lanes]
        parts = []
        for j in range(9):
            keys = blocks[j][:, 0, :, lanes].reshape(ROWS, HEAD_DIM)
            score = lax.dot_general(
                query, keys, (((1,), (1,)), ((), ())), preferred_element_type=jnp.float32
            )
            parts.append(jnp.where(valid_ref[j] > 0, score, NEG))
        scores = jnp.concatenate(parts, axis=-1)
        largest = jnp.max(scores, axis=-1, keepdims=True)
        lifted = jnp.exp2((scores - largest) * EXP2_SCALE)
        total = jnp.sum(lifted, axis=-1, keepdims=True)
        values = jnp.concatenate(
            [blocks[j][:, 1, :, lanes].reshape(ROWS, HEAD_DIM) for j in range(9)], axis=0
        )
        acc_ref[p] = jnp.dot(
            lifted.astype(jnp.bfloat16), values, preferred_element_type=jnp.float32
        )
        lane = lax.broadcasted_iota(jnp.int32, (ROWS, HEAD_DIM), 1)
        stat_ref[p] = jnp.where(lane < HEAD_DIM // 2, largest, total)


def window_attention(valid, queries, blocks):
    steps = HEADS // PAIR
    width = PAIR * HEAD_DIM
    stat = jax.ShapeDtypeStruct((HEADS, ROWS, HEAD_DIM), jnp.float32)
    block = pl.BlockSpec((NW, 2, CUBE, width), lambda i, v: (0, 0, 0, i))
    out = pl.BlockSpec((PAIR, ROWS, HEAD_DIM), lambda i, v: (i, 0, 0))
    return pl.pallas_call(
        window_kernel,
        name="window_attention",
        out_shape=(stat, stat),
        grid_spec=pltpu.PrefetchScalarGridSpec(
            num_scalar_prefetch=1,
            grid=(steps,),
            in_specs=[pl.BlockSpec((ROWS, width), lambda i, v: (0, i))] + [block] * 9,
            out_specs=(out, out),
        ),
        cost_estimate=pl.CostEstimate(
            flops=HEADS * 4 * ROWS * 9 * ROWS * HEAD_DIM,
            bytes_accessed=20_000_000,
            transcendentals=HEADS * ROWS * 9 * ROWS,
        ),
    )(valid, queries, *blocks)


def far_kernel(
    slot_ref, q_ref, tiles_ref, acc_ref, stat_ref, w_ref, out_ref, buf, total, sem
):
    step = pl.program_id(0)
    steps = pl.num_programs(0)
    lists = PAIR * NW

    def fetch(at, into):
        def start(i, carry):
            head = at * PAIR + i // (NW * FAR)
            cube = i // FAR % NW
            slot = slot_ref[(cube * HEADS + head) * FAR + i % FAR]
            pltpu.make_async_copy(
                tiles_ref.at[slot], buf.at[into, i // FAR, i % FAR], sem.at[into]
            ).start()
            return carry

        lax.fori_loop(0, lists * FAR, start, 0)

    @pl.when(step == 0)
    def _():
        fetch(0, 0)
        total[...] = jnp.zeros_like(total)

    now = step % 2

    @pl.when(step + 1 < steps)
    def _():
        fetch(step + 1, 1 - now)

    pltpu.make_async_copy(buf.at[now], buf.at[now], sem.at[now]).wait()
    heads = []
    for p in range(PAIR):
        cubes = []
        for c in range(NW):
            rows = slice(c * CUBE, (c + 1) * CUBE)
            query = q_ref[rows, p * HEAD_DIM : (p + 1) * HEAD_DIM]
            keys = buf[now, p * NW + c, :, 0].reshape(FAR * CUBE, HEAD_DIM)
            values = buf[now, p * NW + c, :, 1].reshape(FAR * CUBE, HEAD_DIM)
            scores = lax.dot_general(
                query, keys, (((1,), (1,)), ((), ())), preferred_element_type=jnp.float32
            )
            near_max = stat_ref[p, rows, 0:1]
            near_sum = stat_ref[p, rows, HEAD_DIM // 2 : HEAD_DIM // 2 + 1]
            largest = jnp.maximum(near_max, jnp.max(scores, axis=-1, keepdims=True))
            lifted = jnp.exp2((scores - largest) * EXP2_SCALE)
            fade = jnp.exp2((near_max - largest) * EXP2_SCALE)
            weight = near_sum * fade + jnp.sum(lifted, axis=-1, keepdims=True)
            summed = acc_ref[p, rows] * fade + jnp.dot(
                lifted.astype(jnp.bfloat16), values, preferred_element_type=jnp.float32
            )
            cubes.append((summed / weight).astype(jnp.bfloat16))
        heads.append(jnp.concatenate(cubes, axis=0))
    attended = jnp.concatenate(heads, axis=1)
    total[...] += jnp.dot(attended, w_ref[...], preferred_element_type=jnp.float32)

    @pl.when(step == steps - 1)
    def _():
        out_ref[...] = total[...].astype(out_ref.dtype)


def far_attention(far_slot, queries, tiles, acc, stat, out_weight):
    steps = HEADS // PAIR
    width = PAIR * HEAD_DIM
    model = queries.shape[1]
    near = pl.BlockSpec((PAIR, ROWS, HEAD_DIM), lambda i, s: (i, 0, 0))
    return pl.pallas_call(
        far_kernel,
        name="far_attention",
        out_shape=jax.ShapeDtypeStruct((ROWS, model), queries.dtype),
        grid_spec=pltpu.PrefetchScalarGridSpec(
            num_scalar_prefetch=1,
            grid=(steps,),
            in_specs=[
                pl.BlockSpec((ROWS, width), lambda i, s: (0, i)),
                pl.BlockSpec(memory_space=pl.ANY),
                near,
                near,
                pl.BlockSpec((width, model), lambda i, s: (i, 0)),
            ],
            out_specs=pl.BlockSpec((ROWS, model), lambda i, s: (0, 0)),
            scratch_shapes=[
                pltpu.VMEM((2, PAIR * NW, FAR, 2, CUBE, HEAD_DIM), queries.dtype),
                pltpu.VMEM((ROWS, model), jnp.float32),
                pltpu.SemaphoreType.DMA((2,)),
            ],
        ),
        cost_estimate=pl.CostEstimate(
            flops=HEADS * 4 * ROWS * FAR * CUBE * HEAD_DIM + 2 * ROWS * model * model,
            bytes_accessed=50_000_000,
            transcendentals=HEADS * ROWS * FAR * CUBE,
        ),
    )(far_slot, queries, tiles, acc, stat, out_weight)


def body(queries, keys_values, far_cubes, out_weight):
    tm_count = lax.axis_size("tm")
    height_count = lax.axis_size("height")
    device_count = tm_count * height_count
    model = queries.shape[-1]
    far = far_cubes.reshape(NW, HEADS, FAR)
    requests, far_slot = request_tables(far, device_count)
    asked = lax.all_to_all(requests, ("tm", "height"), split_axis=0, concat_axis=0, tiled=True)
    kv = keys_values.reshape(NW, 2, CUBE, model)
    tiles = gather_tiles(asked.reshape(SLOTS), kv)
    tiles = lax.all_to_all(tiles, ("tm", "height"), split_axis=0, concat_axis=0, tiled=True)

    def ring(axis, count, by):
        return [(i, (i + by) % count) for i in range(count)]

    column = [
        lax.ppermute(kv, "height", ring("height", height_count, 1)),
        kv,
        lax.ppermute(kv, "height", ring("height", height_count, -1)),
    ]
    blocks = [lax.ppermute(b, "tm", ring("tm", tm_count, 1)) for b in column]
    blocks = blocks + column
    blocks = blocks + [lax.ppermute(b, "tm", ring("tm", tm_count, -1)) for b in column]
    offsets = jnp.arange(3, dtype=jnp.int32) - 1
    times = lax.axis_index("tm") + offsets
    heights = lax.axis_index("height") + offsets
    valid = ((times >= 0) & (times < tm_count))[:, None]
    valid = valid & ((heights >= 0) & (heights < height_count))[None, :]
    valid = valid.reshape(9).astype(jnp.int32)
    flat_queries = queries.reshape(ROWS, model)
    acc, stat = window_attention(valid, flat_queries, blocks)
    output = far_attention(
        far_slot.reshape(NW * HEADS * FAR), flat_queries, tiles, acc, stat, out_weight
    )
    return output.reshape(queries.shape)


def solution(mesh):
    in_specs = (
        P("tm", "height", None, None, None),
        P("tm", "height", None, None, None, None),
        P("tm", "height", None, None, None),
        P(),
    )
    out_specs = P("tm", "height", None, None, None)
    return jax.shard_map(body, mesh=mesh, in_specs=in_specs, out_specs=out_specs, check_vma=False)
```

time: 767 us -> 421 us (0.55)
  the two profiles are of different devices: /device:TPU:1 before, /device:TPU:67 now
where the time goes in v1:
time: 421 us
  waiting for transfers between devices  291 us (69%)
  Pallas kernels  74 us (18%)
  starting transfers between devices  31.2 us (7%)
  blocking collectives  16.8 us (4%)
  local copies, waits for them, and re-layouts  4.99 us (1%)
    ppermute x1, waiting for transfers between devices, body(): lax.ppermute(kv, 'height', ring('height', height_count, 1))  260 us
    pallas_call x1, Pallas kernels, far_attention(): pl.pallas_call(far_kernel, name='far_attention', out_shape=jax.ShapeDtype...  44.5 us
    ppermute x3, waiting for transfers between devices, body(): blocks = [lax.ppermute(b, 'tm', ring('tm', tm_count, 1)) for b in column]  28.9 us
    ppermute x3, starting transfers between devices, body(): blocks = [lax.ppermute(b, 'tm', ring('tm', tm_count, 1)) for b in column]  20.7 us
    pallas_call x1, Pallas kernels, window_attention(): pl.pallas_call(window_kernel, name='window_attention', out_shape=(stat, s...  17.9 us
    all_to_all x1, blocking collectives, body(): lax.all_to_all(requests, ('tm', 'height'), split_axis=0, concat_axis=0, t...  16.8 us
    pallas_call x1, Pallas kernels, gather_tiles(): pl.pallas_call(gather_kernel, name='gather_tiles', out_shape=jax.ShapeDty...  11.6 us
    all_to_all x1, starting transfers between devices, body(): lax.all_to_all(tiles, ('tm', 'height'), split_axis=0, concat_axis=0, tile...  8.92 us
  transfers between devices with their start and end apart: 9, of which 4 were waited for; matrix products, arithmetic and copies ran while one was open for 1% of the time, Pallas kernels for 4%

profile of v1, /device:TPU:67, one launch (start us, length us, event | category | flops | bytes accessed | tf_op | source)
XLA Modules:
  0.0 420.7 jit_solution(5788104555520183114)
XLA Ops:
  0.0 0.8 copy.19
  0.8 0.2 fusion
  1.0 0.1 copy.20
  1.2 0.1 reshape.58
  1.2 0.1 copy.21
  1.3 0.2 broadcast_add_fusion
  1.6 0.1 copy.24
  1.7 16.8 %all_to_all.14 = s32[128,1,4]{2,1,0:T(1,128)S(1)} all-to-all(s32[128,1,4]{2,1,0:T(1,128)S(1)} %copy.24), channel_id=1, replica_groups=mesh['tm'=8,'height'=16] {'tm','height'}, dimensions={0} | all-to-all | bytes 4096 | tf_op jit(solution)/shard_map/all_to_all | solution.py:225
  18.5 0.5 broadcast.66
  19.0 0.8 reduce.3
  19.8 0.7 reshape.63.asked_ref
  20.5 11.6 %gather_tiles.1 = bf16[512,2,64,128]{3,2,1,0:T(8,128)(2,1)} custom-call(s32[512]{0:T(512)} %reshape.63.asked_ref, bf16[2,2,64,3072]{3,2,1,0:T(8,128)(2,1)} %bitcast.14), custom_call_target="tpu_custom_call" | custom-call | bytes 16777216 | tf_op jit(solution)/shard_map/gather_tiles/pallas_call | solution.py:56
  32.1 0.0 copy-start
  32.1 8.9 %all-to-all-start.1 = ((bf16[512,2,64,128]{3,2,1,0:T(8,128)(2,1)}), bf16[512,2,64,128]{3,2,1,0:T(8,128)(2,1)}, u32[]{:S(2)}, u32[]{:S(2)}) async-start(bf16[512,2,64,128]{3,2,1,0:T(8,128)(2,1)} %gather_tiles.1), calls=%async_computation.1 | async-start | bytes 33554432 | tf_op jit(solution)/shard_map/all_to_all | solution.py:228
  41.0 1.3 collective-permute-start
  42.3 0.3 collective-permute-start.3
  42.6 2.1 collective-permute-start.2
  44.6 259.9 %collective-permute-done.refs_3_ = bf16[2,2,64,3072]{3,2,1,0:T(8,128)(2,1)S(1)} collective-permute-done((bf16[2,2,64,3072]{3,2,1,0:T(8,128)(2,1)S(1)}, bf16[2,2,64,3072]{3,2,1,0:T(8,128)(2,1)S(1)}, u32[]{:S(2)}, u32[]{:S(2)}) %collective-permute-start) | collective-permute-done | bytes 1572896 | tf_op jit(solution)/shard_map/ppermute | solution.py:234
  304.6 16.9 %collective-permute-start.1 = (bf16[2,2,64,3072]{3,2,1,0:T(8,128)(2,1)S(1)}, bf16[2,2,64,3072]{3,2,1,0:T(8,128)(2,1)}, u32[]{:S(2)}, u32[]{:S(2)}) collective-permute-start(bf16[2,2,64,3072]{3,2,1,0:T(8,128)(2,1)S(1)} %collective-permute-done.refs_3_), channel_id=1, source_target_pairs={{0,16},{16,32},{32,48},{48,64},{64,80},{80,96},{96,112},{112,0},{1... | collective-permute-start | bytes 4718600 | tf_op jit(solution)/shard_map/ppermute | solution.py:238
  321.5 1.7 collective-permute-start.4
  323.2 1.2 copy-done.2
  324.4 0.1 copy.22
  324.5 0.1 copy.23
  324.6 1.0 select_reduce_fusion
  325.6 0.7 reshape.61.slot_ref
  326.3 0.1 and_convert_fusion
  326.4 0.6 reshape.66.valid_ref
  326.9 11.9 %collective-permute-done.1.refs_0_ = bf16[2,2,64,3072]{3,2,1,0:T(8,128)(2,1)} collective-permute-done((bf16[2,2,64,3072]{3,2,1,0:T(8,128)(2,1)S(1)}, bf16[2,2,64,3072]{3,2,1,0:T(8,128)(2,1)}, u32[]{:S(2)}, u32[]{:S(2)}) %collective-permute-start.1) | collective-permute-done | bytes 1572896 | tf_op jit(solution)/shard_map/ppermute | solution.py:238
  338.8 17.0 %collective-permute-done.4.refs_2_ = bf16[2,2,64,3072]{3,2,1,0:T(8,128)(2,1)} collective-permute-done((bf16[2,2,64,3072]{3,2,1,0:T(8,128)(2,1)}, bf16[2,2,64,3072]{3,2,1,0:T(8,128)(2,1)}, u32[]{:S(2)}, u32[]{:S(2)}) %collective-permute-start.4) | collective-permute-done | bytes 1572896 | tf_op jit(solution)/shard_map/ppermute | solution.py:238
  355.8 2.5 collective-permute-done.7.refs_8_
  358.3 17.9 %window_attention.1 = (f32[24,128,128]{2,1,0:T(8,128)}, f32[24,128,128]{2,1,0:T(8,128)}) custom-call(s32[9]{0:T(128)} %reshape.66.valid_ref, bf16[128,3072]{1,0:T(8,128)(2,1)} %bitcast.20, bf16[2,2,64,3072]{3,2,1,0:T(8,128)(2,1)} %collective-permute-done.1.refs_0_, bf16[2,2,64,3072]{3,2,1,0:T(8,128)(2,1)} %copy-done.2, ...), custom_call_target="tpu_custom_call" | custom-call | flops 1811939328 | bytes 20000000 | tf_op jit(solution)/shard_map/window_attention/pallas_call | solution.py:105
  376.2 44.5 %far_attention.1 = bf16[128,3072]{1,0:T(8,128)(2,1)} custom-call(s32[768]{0:T(1024)} %reshape.61.slot_ref, bf16[128,3072]{1,0:T(8,128)(2,1)} %bitcast.21, bf16[512,2,64,128]{3,2,1,0:T(8,128)(2,1)} %all-to-all-done.1.tiles_ref, f32[24,128,128]{2,1,0:T(8,128)} %get-tuple-element.7.acc_ref, f32[24,128,128]{2,1,0:T(8,128)} %get-tuple-element.8.stat_ref, ...), custom_call_target="tpu_custom_call" | custom-call | flops 4026531840 | bytes 50000000 | tf_op jit(solution)/shard_map/far_attention/pallas_call | solution.py:189
  (15 shorter events, 0.1 us)
Async XLA Ops:
  32.1 8.9 %copy-start = (bf16[1,1,2,2,64,3072]{5,4,3,2,1,0:T(8,128)(2,1)S(1)}, bf16[1,1,2,2,64,3072]{5,4,3,2,1,0:T(8,128)(2,1)}, u32[]{:S(2)}) copy-start(bf16[1,1,2,2,64,3072]{5,4,3,2,1,0:T(8,128)(2,1)} %param.5) | copy-start | bytes 4718596
  32.1 344.1 %all-to-all-start.1 = ((bf16[512,2,64,128]{3,2,1,0:T(8,128)(2,1)}), bf16[512,2,64,128]{3,2,1,0:T(8,128)(2,1)}, u32[]{:S(2)}, u32[]{:S(2)}) async-start(bf16[512,2,64,128]{3,2,1,0:T(8,128)(2,1)} %gather_tiles.1), calls=%async_computation.1 | async-start | bytes 33554432 | tf_op jit(solution)/shard_map/all_to_all | solution.py:228
  41.0 263.5 %collective-permute-start = (bf16[2,2,64,3072]{3,2,1,0:T(8,128)(2,1)S(1)}, bf16[2,2,64,3072]{3,2,1,0:T(8,128)(2,1)S(1)}, u32[]{:S(2)}, u32[]{:S(2)}) collective-permute-start(bf16[2,2,64,3072]{3,2,1,0:T(8,128)(2,1)S(1)} %bitcast.16), channel_id=1, source_target_pairs={{0,1},{1,2},{2,3},{3,4},{4,5},{5,6},{6,7},{7,8},{8,9},{9,10},{10,1... | collective-permute-start | bytes 4718600 | tf_op jit(solution)/shard_map/ppermute | solution.py:234
  42.3 279.2 %collective-permute-start.3 = (bf16[2,2,64,3072]{3,2,1,0:T(8,128)(2,1)S(1)}, bf16[2,2,64,3072]{3,2,1,0:T(8,128)(2,1)}, u32[]{:S(2)}, u32[]{:S(2)}) collective-permute-start(bf16[2,2,64,3072]{3,2,1,0:T(8,128)(2,1)S(1)} %bitcast.17), channel_id=1, source_target_pairs={{0,15},{1,0},{2,1},{3,2},{4,3},{5,4},{6,5},{7,6},{8,7},{9,8},{10,9... | collective-permute-start | bytes 4718600 | tf_op jit(solution)/shard_map/ppermute | solution.py:236
  42.6 280.7 %collective-permute-start.2 = (bf16[2,2,64,3072]{3,2,1,0:T(8,128)(2,1)S(1)}, bf16[2,2,64,3072]{3,2,1,0:T(8,128)(2,1)S(1)}, u32[]{:S(2)}, u32[]{:S(2)}) collective-permute-start(bf16[2,2,64,3072]{3,2,1,0:T(8,128)(2,1)S(1)} %bitcast.18), channel_id=1, source_target_pairs={{0,16},{16,32},{32,48},{48,64},{64,80},{80,96},{96,112},{112,0},{1... | collective-permute-start | bytes 4718600 | tf_op jit(solution)/shard_map/ppermute | solution.py:238
  44.6 282.3 %collective-permute-start.6 = (bf16[2,2,64,3072]{3,2,1,0:T(8,128)(2,1)S(1)}, bf16[2,2,64,3072]{3,2,1,0:T(8,128)(2,1)}, u32[]{:S(2)}, u32[]{:S(2)}) collective-permute-start(bf16[2,2,64,3072]{3,2,1,0:T(8,128)(2,1)S(1)} %bitcast.19), channel_id=1, source_target_pairs={{0,112},{16,0},{32,16},{48,32},{64,48},{80,64},{96,80},{112,96},{1... | collective-permute-start | bytes 4718600 | tf_op jit(solution)/shard_map/ppermute | solution.py:240
  304.6 53.7 %copy-start.1 = (bf16[2,2,64,3072]{3,2,1,0:T(8,128)(2,1)}, bf16[2,2,64,3072]{3,2,1,0:T(8,128)(2,1)S(1)}, u32[]{:S(2)}) copy-start(bf16[2,2,64,3072]{3,2,1,0:T(8,128)(2,1)S(1)} %collective-permute-done.refs_3_) | copy-start | bytes 4718596
  304.6 34.3 %collective-permute-start.1 = (bf16[2,2,64,3072]{3,2,1,0:T(8,128)(2,1)S(1)}, bf16[2,2,64,3072]{3,2,1,0:T(8,128)(2,1)}, u32[]{:S(2)}, u32[]{:S(2)}) collective-permute-start(bf16[2,2,64,3072]{3,2,1,0:T(8,128)(2,1)S(1)} %collective-permute-done.refs_3_), channel_id=1, source_target_pairs={{0,16},{16,32},{32,48},{48,64},{64,80},{80,96},{96,112},{112,0},{1... | collective-permute-start | bytes 4718600 | tf_op jit(solution)/shard_map/ppermute | solution.py:238
  321.5 34.3 %collective-permute-start.5 = (bf16[2,2,64,3072]{3,2,1,0:T(8,128)(2,1)S(1)}, bf16[2,2,64,3072]{3,2,1,0:T(8,128)(2,1)}, u32[]{:S(2)}, u32[]{:S(2)}) collective-permute-start(bf16[2,2,64,3072]{3,2,1,0:T(8,128)(2,1)S(1)} %collective-permute-done.refs_3_), channel_id=1, source_target_pairs={{0,112},{16,0},{32,16},{48,32},{64,48},{80,64},{96,80},{112,96},{1... | collective-permute-start | bytes 4718600 | tf_op jit(solution)/shard_map/ppermute | solution.py:240
  321.5 34.3 %collective-permute-start.4 = (bf16[2,2,64,3072]{3,2,1,0:T(8,128)(2,1)}, bf16[2,2,64,3072]{3,2,1,0:T(8,128)(2,1)}, u32[]{:S(2)}, u32[]{:S(2)}) collective-permute-start(bf16[2,2,64,3072]{3,2,1,0:T(8,128)(2,1)} %collective-permute-done.3.refs_5_), channel_id=1, source_target_pairs={{0,16},{16,32},{32,48},{48,64},{64,80},{80,96},{96,112},{112,0},{1... | collective-permute-start | bytes 4718600 | tf_op jit(solution)/shard_map/ppermute | solution.py:238
  323.2 1.2 copy-start.2
  324.4 33.9 %collective-permute-start.7 = (bf16[2,2,64,3072]{3,2,1,0:T(8,128)(2,1)}, bf16[2,2,64,3072]{3,2,1,0:T(8,128)(2,1)}, u32[]{:S(2)}, u32[]{:S(2)}) collective-permute-start(bf16[2,2,64,3072]{3,2,1,0:T(8,128)(2,1)} %collective-permute-done.3.refs_5_), channel_id=1, source_target_pairs={{0,112},{16,0},{32,16},{48,32},{64,48},{80,64},{96,80},{112,96},{1... | collective-permute-start | bytes 4718600 | tf_op jit(solution)/shard_map/ppermute | solution.py:240

commit v2 on v1

v2 whole, which is shorter than its diff:
```python
import functools
import math

import jax
import jax.numpy as jnp
from jax import lax
from jax.experimental import pallas as pl
from jax.experimental.pallas import tpu as pltpu
from jax.sharding import PartitionSpec as P

HEADS = 24
HEAD_DIM = 128
CUBE = 64
FAR = 16
NW = 2
SLOTS = 512
PAIR = 2
ROWS = NW * CUBE
NEG = -1e30
EXP2_SCALE = math.log2(math.e) / math.sqrt(HEAD_DIM)


def request_tables(far, device_count):
    capacity = SLOTS // device_count
    cubes = device_count * NW
    hit = far[:, :, :, None] == jnp.arange(cubes, dtype=jnp.int32)
    wanted = jnp.any(hit, axis=(0, 2))
    wanted = jnp.transpose(wanted.reshape(HEADS, device_count, NW), (1, 2, 0))
    wanted = wanted.reshape(device_count, NW * HEADS)
    codes = jnp.arange(NW * HEADS, dtype=jnp.int32)
    before = (codes[:, None] < codes[None, :]).astype(jnp.bfloat16)
    rank = jnp.dot(wanted.astype(jnp.bfloat16), before, preferred_element_type=jnp.float32)
    rank = rank.astype(jnp.int32)
    chosen = wanted[:, :, None] & (rank[:, :, None] == jnp.arange(2 * capacity, dtype=jnp.int32))
    labels = codes // HEADS * 32 + codes % HEADS
    requests = jnp.sum(jnp.where(chosen, labels[None, :, None], 0), axis=1)
    slot = rank + jnp.arange(device_count, dtype=jnp.int32)[:, None] * capacity
    slot = jnp.transpose(slot.reshape(device_count, NW, HEADS), (2, 0, 1)).reshape(HEADS, cubes)
    far_slot = jnp.sum(jnp.where(hit, slot[None, :, None, :], 0), axis=-1)
    rank, owner = far_slot % capacity, far_slot // capacity
    y, k, z, x = owner // 32, owner // 16 % 2, owner // 4 % 4, owner % 4
    in_x = (((y * 4 + z) * 2 + k) * 4 + x) * capacity + rank
    in_y = (((z * 4 + x) * 2 + k) * 4 + y) * capacity + rank
    in_z = (((x * 4 + y) * 2 + k) * 4 + z) * capacity + rank
    return requests.T, in_x + in_y * SLOTS + in_z * SLOTS * SLOTS


PART_ROWS = (48, 48, 32)
PIECES = (
    ((0, 0, 48, 0),),
    ((0, 48, 64, 0), (1, 0, 32, 16)),
    ((1, 32, 64, 0),),
)
AXES = ("x", "y", "z")
MESH = pl.DeviceIdType.MESH


def position():
    t, h = lax.axis_index("tm"), lax.axis_index("height")
    return {"x": h % 4, "y": t // 2, "z": h // 4, "k": t % 2}


def device(at):
    return at["y"] * 2 + at["k"], at["z"] * 4 + at["x"]


def moved(at, **by):
    return {n: (v + by.get(n, 0)) % (2 if n == "k" else 4) for n, v in at.items()}


def greet(peers):
    barrier = pltpu.get_barrier_semaphore()
    for peer in peers:
        pl.semaphore_signal(barrier, inc=1, device_id=peer, device_id_type=MESH)
    pl.semaphore_wait(barrier, len(peers))


def spread_kernel(
    kv_ref,
    table_ref,
    window_ref,
    rows0_ref,
    rows1_ref,
    rows2_ref,
    tables_ref,
    local_sem,
    send_sem,
    window_sem,
    rows_sem,
    table_sem,
):
    me = position()
    t, h = lax.axis_index("tm"), lax.axis_index("height")
    rows_refs = (rows0_ref, rows1_ref, rows2_ref)
    later, earlier = (t, (h + 1) % 16), (t, (h + 15) % 16)
    after, before = ((t + 1) % 8, h), ((t + 7) % 8, h)
    peers = [later, earlier, after, before]
    peers += [device(moved(me, **{a: d})) for a in AXES for d in (1, 2, 3)]
    peers += [device(moved(me, k=1))]
    greet(peers)
    sent = []

    def send(src, dst, sem, to):
        copy = pltpu.make_async_remote_copy(
            src_ref=src,
            dst_ref=dst,
            send_sem=send_sem.at[len(sent)],
            recv_sem=sem,
            device_id=to,
            device_id_type=MESH,
        )
        copy.start()
        sent.append(copy)
        return copy

    own_table = tables_ref.at[me["k"], me["z"], me["y"], me["x"]]
    copies = [pltpu.make_async_copy(table_ref, own_table, local_sem.at[0])]
    for part in range(3):
        for n, (kind, low, high, at) in enumerate(PIECES[part]):
            copies.append(
                pltpu.make_async_copy(
                    kv_ref.at[:, kind, low:high],
                    rows_refs[part].at[me[AXES[part]], :, at : at + high - low],
                    local_sem.at[1 + part * 2 + n],
                )
            )
    for copy in copies:
        copy.start()

    def tables(stage, src, dst):
        axis = "xyzk"[stage]
        return [
            send(src, dst, table_sem.at[stage, d - 1], device(moved(me, **{axis: d})))
            for d in range(1, 2 if axis == "k" else 4)
        ]

    table_x = tables(0, table_ref, own_table)
    from_earlier = send(kv_ref, window_ref.at[1, 0], window_sem.at[0], later)
    from_later = send(kv_ref, window_ref.at[1, 2], window_sem.at[1], earlier)
    windows = [
        send(kv_ref, window_ref.at[0, 1], window_sem.at[2], after),
        send(kv_ref, window_ref.at[2, 1], window_sem.at[3], before),
    ]
    near = []
    for part in range(3):
        for way, d in enumerate((1, 3)):
            group = []
            for n, (kind, low, high, at) in enumerate(PIECES[part]):
                group.append(
                    send(
                        kv_ref.at[:, kind, low:high],
                        rows_refs[part].at[me[AXES[part]], :, at : at + high - low],
                        rows_sem.at[part, way, n],
                        device(moved(me, **{AXES[part]: d})),
                    )
                )
            near.append(group)
    copies[0].wait()
    for copy in table_x:
        copy.wait_recv()
    row = tables_ref.at[me["k"], me["z"], me["y"]]
    table_y = tables(1, row, row)
    for copy in table_y:
        copy.wait_recv()
    plane = tables_ref.at[me["k"], me["z"]]
    table_z = tables(2, plane, plane)
    for copy in table_z:
        copy.wait_recv()
    core = tables_ref.at[me["k"]]
    table_k = tables(3, core, core)
    far = []
    for part in (2, 1, 0):
        for way, d in enumerate((1, 3)):
            for copy in near[part * 2 + way]:
                copy.wait_recv()
            block = rows_refs[part].at[moved(me, **{AXES[part]: 4 - d})[AXES[part]], way]
            far.append(
                send(
                    block,
                    block,
                    rows_sem.at[part, 2 + way, 0],
                    device(moved(me, **{AXES[part]: d})),
                )
            )
    for j, copy in ((0, from_earlier), (2, from_later)):
        copy.wait_recv()
        block = window_ref.at[1, j]
        windows.append(send(block, window_ref.at[0, j], window_sem.at[4 + j], after))
        windows.append(send(block, window_ref.at[2, j], window_sem.at[5 + j], before))
    for copy in table_k + far + windows:
        copy.wait_recv()
    for copy in copies[1:]:
        copy.wait()
    for copy in sent:
        copy.wait_send()


def spread(kv, table):
    width = kv.shape[-1]
    hbm = pl.BlockSpec(memory_space=pl.ANY)
    vmem = pl.BlockSpec(memory_space=pltpu.VMEM)
    rows = [jax.ShapeDtypeStruct((4, NW, r, width), kv.dtype) for r in PART_ROWS]
    return pl.pallas_call(
        spread_kernel,
        name="spread",
        out_shape=(
            jax.ShapeDtypeStruct((3, 3) + kv.shape, kv.dtype),
            *rows,
            jax.ShapeDtypeStruct((2, 4, 4, 4) + table.shape, table.dtype),
        ),
        in_specs=[vmem, vmem],
        out_specs=(hbm,) * 5,
        scratch_shapes=[
            pltpu.SemaphoreType.DMA((7,)),
            pltpu.SemaphoreType.DMA((40,)),
            pltpu.SemaphoreType.DMA((8,)),
            pltpu.SemaphoreType.DMA((3, 4, 2)),
            pltpu.SemaphoreType.DMA((4, 3)),
        ],
        compiler_params=pltpu.CompilerParams(collective_id=0, has_side_effects=True),
    )(kv, table)


def pick_kernel(code0, code1, code2, rows0, rows1, rows2, out0, out1, out2):
    step = pl.program_id(0) * 4 + pl.program_id(1)
    tiles = 32

    def one(i, carry):
        for code_ref, rows, out in ((code0, rows0, out0), (code1, rows1, out1), (code2, rows2, out2)):
            code = code_ref[step * tiles + i]
            lane = pl.multiple_of((code & 31) * HEAD_DIM, HEAD_DIM)
            out[0, 0, i] = rows[(i >> 2) & 3, code >> 5, :, pl.ds(lane, HEAD_DIM)]
        return carry

    lax.fori_loop(0, tiles, one, 0, unroll=8)


def pick(codes, rows):
    shapes = [(4, 4, 32, r, HEAD_DIM) for r in PART_ROWS]
    return pl.pallas_call(
        pick_kernel,
        name="pick_tiles",
        out_shape=[jax.ShapeDtypeStruct(s, rows[0].dtype) for s in shapes],
        grid_spec=pltpu.PrefetchScalarGridSpec(
            num_scalar_prefetch=3,
            grid=(4, 4),
            in_specs=[
                pl.BlockSpec(r.shape, lambda i, j, *c: (0, 0, 0, 0), pipeline_mode=pl.Buffered(1))
                for r in rows
            ],
            out_specs=[
                pl.BlockSpec((1, 1) + s[2:], lambda i, j, *c: (i, j, 0, 0, 0)) for s in shapes
            ],
        ),
    )(*codes, *rows)


def exchange_kernel(*refs):
    picked, got, between = refs[:3], refs[3:6], refs[6:9]
    local_sem, send_sem, mid_sem, last_sem = refs[9:]
    me = position()
    routes = [("x", "y", "z"), ("y", "z", "x"), ("z", "x", "y")]
    peers = []
    for axis in AXES:
        for d in (1, 2, 3):
            for k in (0, 1):
                peers.append(device(moved(me, **{axis: d}, k=k)))
    peers.append(device(moved(me, k=1)))
    greet(peers)
    middle = []
    for part in range(3):
        second = routes[part][1]
        group = []
        for n, d in enumerate((1, 3, 2)):
            to = moved(me, **{second: d})
            copy = pltpu.make_async_remote_copy(
                src_ref=picked[part].at[to[second]],
                dst_ref=between[part].at[me[second]],
                send_sem=send_sem.at[part, 0],
                recv_sem=mid_sem.at[part, n],
                device_id=device(to),
                device_id_type=MESH,
            )
            copy.start()
            group.append(copy)
        middle.append(group)
    for n, d in enumerate((0, 3, 1, 2)):
        for part in range(3):
            _, second, third = routes[part]
            came = moved(me, **{second: d})[second]
            if n > 0:
                middle[part][n - 1].wait_recv()
                held = between[part].at[came]
            else:
                held = picked[part].at[came]
            for e in (1, 3, 2, 0):
                for k in (0, 1):
                    to = moved(me, **{third: e}, k=k)
                    src = held.at[to[third], pl.ds(to["k"] * 16, 16)]
                    dst = got[part].at[came, me[third], me["k"]]
                    if e == 0 and k == 0:
                        pltpu.make_async_copy(src, dst, local_sem.at[part]).start()
                    else:
                        pltpu.make_async_remote_copy(
                            src_ref=src,
                            dst_ref=dst,
                            send_sem=send_sem.at[part, 1],
                            recv_sem=last_sem.at[part],
                            device_id=device(to),
                            device_id_type=MESH,
                        ).start()
    for part in range(3):
        whole = got[part].at[:, :, :, 0:14]
        pltpu.make_async_copy(whole, whole, last_sem.at[part]).wait()
        pltpu.make_async_copy(whole, whole, send_sem.at[part, 1]).wait()
        some = got[part].at[:, 0, 0]
        pltpu.make_async_copy(some, some, local_sem.at[part]).wait()
        some = between[part].at[0:3]
        pltpu.make_async_copy(some, some, send_sem.at[part, 0]).wait()


def exchange(picked):
    hbm = pl.BlockSpec(memory_space=pl.ANY)
    got = [jax.ShapeDtypeStruct((4, 4, 2, 16, r, HEAD_DIM), picked[0].dtype) for r in PART_ROWS]
    between = [jax.ShapeDtypeStruct(p.shape, p.dtype) for p in picked]
    outs = pl.pallas_call(
        exchange_kernel,
        name="exchange",
        out_shape=got + between,
        in_specs=[hbm] * 3,
        out_specs=[hbm] * 6,
        scratch_shapes=[
            pltpu.SemaphoreType.DMA((3,)),
            pltpu.SemaphoreType.DMA((3, 2)),
            pltpu.SemaphoreType.DMA((3, 3)),
            pltpu.SemaphoreType.DMA((3,)),
        ],
        compiler_params=pltpu.CompilerParams(collective_id=1, has_side_effects=True),
    )(*picked)
    return [g.reshape(SLOTS, r, HEAD_DIM) for g, r in zip(outs[:3], PART_ROWS)]


def asked_codes(tables):
    at = position()
    t = tables.reshape(2, 4, 4, 4, 8, 4, 2, 4, 4)[:, :, :, :, :4]
    t = lax.dynamic_index_in_dim(t, at["k"], 6, keepdims=False)

    def take(value, which):
        for axis, name in which:
            value = lax.dynamic_index_in_dim(value, at[name], axis, keepdims=True)
        return value

    part0 = take(t, ((3, "x"), (5, "y"), (6, "z")))[:, :, :, 0, :, 0, 0, :]
    part1 = take(t, ((2, "y"), (6, "z"), (7, "x")))[:, :, 0, :, :, :, 0, 0]
    part2 = take(t, ((1, "z"), (5, "y"), (7, "x")))[:, 0, :, :, :, 0, :, 0]
    return [
        jnp.transpose(part0, (2, 1, 0, 4, 3)).reshape(SLOTS),
        jnp.transpose(part1, (1, 2, 0, 4, 3)).reshape(SLOTS),
        jnp.transpose(part2, (2, 1, 0, 4, 3)).reshape(SLOTS),
    ]


def window_kernel(valid_ref, q_ref, *refs):
    own_ref, window_ref, acc_ref, stat_ref = refs

    def block(j, kind, lanes):
        if j == 4:
            return own_ref[:, kind, :, lanes].reshape(ROWS, HEAD_DIM)
        return window_ref[j // 3, j % 3, :, kind, :, lanes].reshape(ROWS, HEAD_DIM)

    for p in range(PAIR):
        lanes = slice(p * HEAD_DIM, (p + 1) * HEAD_DIM)
        query = q_ref[:, lanes]
        parts = []
        for j in range(9):
            keys = block(j, 0, lanes)
            score = lax.dot_general(
                query, keys, (((1,), (1,)), ((), ())), preferred_element_type=jnp.float32
            )
            parts.append(jnp.where(valid_ref[j] > 0, score, NEG))
        scores = jnp.concatenate(parts, axis=-1)
        largest = jnp.max(scores, axis=-1, keepdims=True)
        lifted = jnp.exp2((scores - largest) * EXP2_SCALE)
        total = jnp.sum(lifted, axis=-1, keepdims=True)
        values = jnp.concatenate(
            [block(j, 1, lanes) for j in range(9)], axis=0
        )
        acc_ref[p] = jnp.dot(
            lifted.astype(jnp.bfloat16), values, preferred_element_type=jnp.float32
        )
        lane = lax.broadcasted_iota(jnp.int32, (ROWS, HEAD_DIM), 1)
        stat_ref[p] = jnp.where(lane < HEAD_DIM // 2, largest, total)


def window_attention(valid, queries, kv, window):
    steps = HEADS // PAIR
    width = PAIR * HEAD_DIM
    stat = jax.ShapeDtypeStruct((HEADS, ROWS, HEAD_DIM), jnp.float32)
    block = pl.BlockSpec((NW, 2, CUBE, width), lambda i, v: (0, 0, 0, i))
    out = pl.BlockSpec((PAIR, ROWS, HEAD_DIM), lambda i, v: (i, 0, 0))
    return pl.pallas_call(
        window_kernel,
        name="window_attention",
        out_shape=(stat, stat),
        grid_spec=pltpu.PrefetchScalarGridSpec(
            num_scalar_prefetch=1,
            grid=(steps,),
            in_specs=[
                pl.BlockSpec((ROWS, width), lambda i, v: (0, i)),
                block,
                pl.BlockSpec((3, 3, NW, 2, CUBE, width), lambda i, v: (0, 0, 0, 0, 0, i)),
            ],
            out_specs=(out, out),
        ),
        cost_estimate=pl.CostEstimate(
            flops=HEADS * 4 * ROWS * 9 * ROWS * HEAD_DIM,
            bytes_accessed=20_000_000,
            transcendentals=HEADS * ROWS * 9 * ROWS,
        ),
    )(valid, queries, kv, window)


def far_kernel(
    slot_ref, q_ref, tiles0, tiles1, tiles2, acc_ref, stat_ref, w_ref, out_ref, total
):
    step = pl.program_id(0)
    steps = pl.num_programs(0)

    @pl.when(step == 0)
    def _():
        total[...] = jnp.zeros_like(total)

    heads = []
    for p in range(PAIR):
        cubes = []
        for c in range(NW):
            rows = slice(c * CUBE, (c + 1) * CUBE)
            query = q_ref[rows, p * HEAD_DIM : (p + 1) * HEAD_DIM]
            keys, values = [], []
            for f in range(FAR):
                slot = slot_ref[(c * HEADS + step * PAIR + p) * FAR + f]
                in0, in1, in2 = slot & (SLOTS - 1), (slot >> 9) & (SLOTS - 1), slot >> 18
                keys += [tiles0[in0], tiles1[in1, 0:16]]
                values += [tiles1[in1, 16:48], tiles2[in2]]
            keys = jnp.concatenate(keys, axis=0)
            values = jnp.concatenate(values, axis=0)
            scores = lax.dot_general(
                query, keys, (((1,), (1,)), ((), ())), preferred_element_type=jnp.float32
            )
            near_max = stat_ref[p, rows, 0:1]
            near_sum = stat_ref[p, rows, HEAD_DIM // 2 : HEAD_DIM // 2 + 1]
            largest = jnp.maximum(near_max, jnp.max(scores, axis=-1, keepdims=True))
            lifted = jnp.exp2((scores - largest) * EXP2_SCALE)
            fade = jnp.exp2((near_max - largest) * EXP2_SCALE)
            weight = near_sum * fade + jnp.sum(lifted, axis=-1, keepdims=True)
            summed = acc_ref[p, rows] * fade + jnp.dot(
                lifted.astype(jnp.bfloat16), values, preferred_element_type=jnp.float32
            )
            cubes.append((summed / weight).astype(jnp.bfloat16))
        heads.append(jnp.concatenate(cubes, axis=0))
    attended = jnp.concatenate(heads, axis=1)
    total[...] += jnp.dot(attended, w_ref[...], preferred_element_type=jnp.float32)

    @pl.when(step == steps - 1)
    def _():
        out_ref[...] = total[...].astype(out_ref.dtype)


def far_attention(far_slot, queries, tiles, acc, stat, out_weight):
    steps = HEADS // PAIR
    width = PAIR * HEAD_DIM
    model = queries.shape[1]
    near = pl.BlockSpec((PAIR, ROWS, HEAD_DIM), lambda i, s: (i, 0, 0))
    return pl.pallas_call(
        far_kernel,
        name="far_attention",
        out_shape=jax.ShapeDtypeStruct((ROWS, model), queries.dtype),
        grid_spec=pltpu.PrefetchScalarGridSpec(
            num_scalar_prefetch=1,
            grid=(steps,),
            in_specs=[
                pl.BlockSpec((ROWS, width), lambda i, s: (0, i)),
                *[
                    pl.BlockSpec(x.shape, lambda i, s: (0, 0, 0), pipeline_mode=pl.Buffered(1))
                    for x in tiles
                ],
                near,
                near,
                pl.BlockSpec((width, model), lambda i, s: (i, 0)),
            ],
            out_specs=pl.BlockSpec((ROWS, model), lambda i, s: (0, 0)),
            scratch_shapes=[pltpu.VMEM((ROWS, model), jnp.float32)],
        ),
        cost_estimate=pl.CostEstimate(
            flops=HEADS * 4 * ROWS * FAR * CUBE * HEAD_DIM + 2 * ROWS * model * model,
            bytes_accessed=50_000_000,
            transcendentals=HEADS * ROWS * FAR * CUBE,
        ),
    )(far_slot, queries, *tiles, acc, stat, out_weight)


def body(queries, keys_values, far_cubes, out_weight):
    tm_count = lax.axis_size("tm")
    height_count = lax.axis_size("height")
    device_count = tm_count * height_count
    model = queries.shape[-1]
    far = far_cubes.reshape(NW, HEADS, FAR)
    requests, far_slot = request_tables(far, device_count)
    kv = keys_values.reshape(NW, 2, CUBE, model)
    window, *rows, tables = spread(kv, requests)
    tiles = exchange(pick(asked_codes(tables), rows))
    offsets = jnp.arange(3, dtype=jnp.int32) - 1
    times = lax.axis_index("tm") + offsets
    heights = lax.axis_index("height") + offsets
    valid = ((times >= 0) & (times < tm_count))[:, None]
    valid = valid & ((heights >= 0) & (heights < height_count))[None, :]
    valid = valid.reshape(9).astype(jnp.int32)
    flat_queries = queries.reshape(ROWS, model)
    acc, stat = window_attention(valid, flat_queries, kv, window)
    output = far_attention(
        far_slot.reshape(NW * HEADS * FAR), flat_queries, tiles, acc, stat, out_weight
    )
    return output.reshape(queries.shape)


def solution(mesh):
    in_specs = (
        P("tm", "height", None, None, None),
        P("tm", "height", None, None, None, None),
        P("tm", "height", None, None, None),
        P(),
    )
    out_specs = P("tm", "height", None, None, None)
    return jax.shard_map(body, mesh=mesh, in_specs=in_specs, out_specs=out_specs, check_vma=False)
```

time: 421 us -> 323 us (0.77)
  the two profiles are of different devices: /device:TPU:67 before, /device:TPU:1 now
where the time goes in v2:
time: 323 us
  Pallas kernels  308 us (95%)
  local copies, waits for them, and re-layouts  11.7 us (4%)
    pallas_call x1, Pallas kernels, exchange(): pl.pallas_call(exchange_kernel, name='exchange', out_shape=got + between,...  143 us
    pallas_call x1, Pallas kernels, spread(): pl.pallas_call(spread_kernel, name='spread', out_shape=(jax.ShapeDtypeStr...  97.2 us
    pallas_call x1, Pallas kernels, far_attention(): pl.pallas_call(far_kernel, name='far_attention', out_shape=jax.ShapeDtype...  35 us
    pallas_call x1, Pallas kernels, window_attention(): pl.pallas_call(window_kernel, name='window_attention', out_shape=(stat, s...  18.2 us
    pallas_call x1, Pallas kernels, pick(): pl.pallas_call(pick_kernel, name='pick_tiles', out_shape=[jax.ShapeDtypeS...  15 us

profile of v2, /device:TPU:1, one launch (start us, length us, event | category | flops | bytes accessed | tf_op | source)
XLA Modules:
  0.0 322.7 jit_solution(6477502947104203855)
XLA Ops:
  0.0 0.1 and_convert_fusion
  0.1 0.7 reshape.116.valid_ref
  0.8 0.8 copy.31
  1.6 0.2 fusion
  1.8 0.1 copy.32
  1.9 0.1 reshape.103
  2.0 0.1 copy.33
  2.1 0.2 broadcast_add_fusion
  2.3 0.7 select_reduce_fusion.1
  3.0 0.1 copy.34
  3.1 0.1 copy.35
  3.2 1.0 select_reduce_fusion
  4.2 0.1 reduce_sum.21
  4.3 0.6 multiply_add_fusion.slot_ref
  4.9 97.2 %spread.1 = (bf16[3,3,2,2,64,3072]{5,4,3,2,1,0:T(8,128)(2,1)}, bf16[4,2,48,3072]{3,2,1,0:T(8,128)(2,1)}, bf16[4,2,48,3072]{3,2,1,0:T(8,128)(2,1)}, bf16[4,2,32,3...) custom-call(bf16[2,2,64,3072]{3,2,1,0:T(8,128)(2,1)} %bitcast.36, s32[8,128]{1,0:T(8,128)} %bitcast.50), custom_call_target="tpu_custom_call" | custom-call | tf_op jit(solution)/shard_map/spread/pallas_call | solution.py:203
  102.2 0.0 copy-start
  102.2 18.2 %window_attention.1 = (f32[24,128,128]{2,1,0:T(8,128)}, f32[24,128,128]{2,1,0:T(8,128)}) custom-call(s32[9]{0:T(128)} %reshape.116.valid_ref, bf16[128,3072]{1,0:T(8,128)(2,1)} %bitcast.41, bf16[2,2,64,3072]{3,2,1,0:T(8,128)(2,1)} %bitcast.37, bf16[3,3,2,2,64,3072]{5,4,3,2,1,0:T(8,128)(2,1)} %get-tuple-element.28.refs_1_), custom_call_target="tpu_custom_call" | custom-call | flops 1811939328 | bytes 20000000 | tf_op jit(solution)/shard_map/window_attention/pallas_call | solution.py:401
  120.3 0.0 copy-done
  120.3 4.6 %copy.36 = s32[2,4,4,4,8,128]{4,5,3,2,1,0:T(8,128)} copy(s32[2,4,4,4,8,128]{5,4,3,2,1,0:T(8,128)S(1)} %copy-done) | data formatting | bytes 1048576 | tf_op jit(solution)/shard_map/spread/pallas_call | solution.py:203
  124.9 1.0 constant_dynamic-slice_fusion.1
  126.0 0.7 reshape.111.code2
  126.7 1.0 constant_dynamic-slice_fusion
  127.7 0.9 dynamic-slice_bitcast_fusion
  128.6 0.7 reshape.109.code0
  129.3 0.7 reshape.110.code1
  130.0 15.0 %pick_tiles.1 = (bf16[4,4,32,48,128]{4,3,2,1,0:T(8,128)(2,1)}, bf16[4,4,32,48,128]{4,3,2,1,0:T(8,128)(2,1)}, bf16[4,4,32,32,128]{4,3,2,1,0:T(8,128)(2,1)}) custom-call(s32[512]{0:T(512)} %reshape.109.code0, s32[512]{0:T(512)} %reshape.110.code1, s32[512]{0:T(512)} %reshape.111.code2, bf16[4,2,48,3072]{3,2,1,0:T(8,128)(2,1)} %get-tuple-element.19.rows0, ...), custom_call_target="tpu_custom_call" | custom-call | tf_op jit(solution)/shard_map/pick_tiles/pallas_call | solution.py:240
  145.0 142.7 %exchange.1 = (bf16[4,4,2,16,48,128]{5,4,3,2,1,0:T(8,128)(2,1)}, bf16[4,4,2,16,48,128]{5,4,3,2,1,0:T(8,128)(2,1)}, bf16[4,4,2,16,32,128]{5,4,3,2,1,0:T(8,128)(2,...) custom-call(bf16[4,4,32,48,128]{4,3,2,1,0:T(8,128)(2,1)} %get-tuple-, ...), custom_call_target="tpu_custom_call" | custom-call | tf_op jit(solution)/shard_map/exchange/pallas_call | solution.py:326
  287.7 35.0 %far_attention.1 = bf16[128,3072]{1,0:T(8,128)(2,1)} custom-call(s32[768]{0:T(1024)} %multiply_add_fusion.slot_ref, bf16[128,3072]{1,0:T(8,128)(2,1)} %bitcast.42, bf16[512,48,128]{2,1,0:T(8,128)(2,1)} %bitcast.38, bf16[512,48,128]{2,1,0:T(8,128)(2,1)} %bitcast.39, bf16[512,32,128]{2,1,0:T(8,128)(2,1)} %bitcast.40, ...), custom_call_target="tpu_custom_call" | custom-call | flops 4026531840 | bytes 50000000 | tf_op jit(solution)/shard_map/far_attention/pallas_call | solution.py:474
  (6 shorter events, 0.1 us)
Async XLA Ops:
  102.2 18.2 %copy-start = (s32[2,4,4,4,8,128]{5,4,3,2,1,0:T(8,128)S(1)}, s32[2,4,4,4,8,128]{5,4,3,2,1,0:T(8,128)}, u32[]{:S(2)}) copy-start(s32[2,4,4,4,8,128]{5,4,3,2,1,0:T(8,128)} %get-tuple-element.18) | copy-start | bytes 1572868

commit v3 on v2

--- a/solution.py
+++ b/solution.py
@@ -78,24 +78,18 @@
 def spread_kernel(
     kv_ref,
     table_ref,
-    window_ref,
     rows0_ref,
     rows1_ref,
     rows2_ref,
     tables_ref,
     local_sem,
     send_sem,
-    window_sem,
     rows_sem,
     table_sem,
 ):
     me = position()
-    t, h = lax.axis_index("tm"), lax.axis_index("height")
     rows_refs = (rows0_ref, rows1_ref, rows2_ref)
-    later, earlier = (t, (h + 1) % 16), (t, (h + 15) % 16)
-    after, before = ((t + 1) % 8, h), ((t + 7) % 8, h)
-    peers = [later, earlier, after, before]
-    peers += [device(moved(me, **{a: d})) for a in AXES for d in (1, 2, 3)]
+    peers = [device(moved(me, **{a: d})) for a in AXES for d in (1, 2, 3)]
     peers += [device(moved(me, k=1))]
     greet(peers)
     sent = []
@@ -134,15 +128,8 @@
             for d in range(1, 2 if axis == "k" else 4)
         ]
 
-    table_x = tables(0, table_ref, own_table)
-    from_earlier = send(kv_ref, window_ref.at[1, 0], window_sem.at[0], later)
-    from_later = send(kv_ref, window_ref.at[1, 2], window_sem.at[1], earlier)
-    windows = [
-        send(kv_ref, window_ref.at[0, 1], window_sem.at[2], after),
-        send(kv_ref, window_ref.at[2, 1], window_sem.at[3], before),
-    ]
-    near = []
-    for part in range(3):
+    def nearest(part):
+        groups = []
         for way, d in enumerate((1, 3)):
             group = []
             for n, (kind, low, high, at) in enumerate(PIECES[part]):
@@ -154,24 +141,30 @@
                         device(moved(me, **{AXES[part]: d})),
                     )
                 )
-            near.append(group)
+            groups.append(group)
+        return groups
+
+    table_x = tables(0, table_ref, own_table)
+    near = [nearest(0)]
     copies[0].wait()
     for copy in table_x:
         copy.wait_recv()
     row = tables_ref.at[me["k"], me["z"], me["y"]]
     table_y = tables(1, row, row)
+    near.append(nearest(1))
     for copy in table_y:
         copy.wait_recv()
     plane = tables_ref.at[me["k"], me["z"]]
     table_z = tables(2, plane, plane)
+    near.append(nearest(2))
     for copy in table_z:
         copy.wait_recv()
     core = tables_ref.at[me["k"]]
     table_k = tables(3, core, core)
     far = []
-    for part in (2, 1, 0):
+    for part in (0, 1, 2):
         for way, d in enumerate((1, 3)):
-            for copy in near[part * 2 + way]:
+            for copy in near[part][way]:
                 copy.wait_recv()
             block = rows_refs[part].at[moved(me, **{AXES[part]: 4 - d})[AXES[part]], way]
             far.append(
@@ -182,12 +175,7 @@
                     device(moved(me, **{AXES[part]: d})),
                 )
             )
-    for j, copy in ((0, from_earlier), (2, from_later)):
-        copy.wait_recv()
-        block = window_ref.at[1, j]
-        windows.append(send(block, window_ref.at[0, j], window_sem.at[4 + j], after))
-        windows.append(send(block, window_ref.at[2, j], window_sem.at[5 + j], before))
-    for copy in table_k + far + windows:
+    for copy in table_k + far:
         copy.wait_recv()
     for copy in copies[1:]:
         copy.wait()
@@ -204,16 +192,14 @@
         spread_kernel,
         name="spread",
         out_shape=(
-            jax.ShapeDtypeStruct((3, 3) + kv.shape, kv.dtype),
             *rows,
             jax.ShapeDtypeStruct((2, 4, 4, 4) + table.shape, table.dtype),
         ),
         in_specs=[vmem, vmem],
-        out_specs=(hbm,) * 5,
+        out_specs=(hbm,) * 4,
         scratch_shapes=[
             pltpu.SemaphoreType.DMA((7,)),
-            pltpu.SemaphoreType.DMA((40,)),
-            pltpu.SemaphoreType.DMA((8,)),
+            pltpu.SemaphoreType.DMA((32,)),
             pltpu.SemaphoreType.DMA((3, 4, 2)),
             pltpu.SemaphoreType.DMA((4, 3)),
         ],
@@ -255,18 +241,69 @@
     )(*codes, *rows)
 
 
+def window_heads(i, valid, q_ref, own_ref, window_ref, acc_ref, stat_ref):
+    def block(j, kind, lanes):
+        ref = own_ref if j == 4 else window_ref.at[j // 3, j % 3]
+        return ref[:, kind, :, lanes].reshape(ROWS, HEAD_DIM)
+
+    for p in range(PAIR):
+        head = i * PAIR + p
+        lanes = pl.ds(pl.multiple_of(head * HEAD_DIM, HEAD_DIM), HEAD_DIM)
+        query = q_ref[:, lanes]
+        parts = []
+        for j in range(9):
+            keys = block(j, 0, lanes)
+            score = lax.dot_general(
+                query, keys, (((1,), (1,)), ((), ())), preferred_element_type=jnp.float32
+            )
+            parts.append(jnp.where(valid[j] > 0, score, NEG))
+        scores = jnp.concatenate(parts, axis=-1)
+        largest = jnp.max(scores, axis=-1, keepdims=True)
+        lifted = jnp.exp2((scores - largest) * EXP2_SCALE)
+        total = jnp.sum(lifted, axis=-1, keepdims=True)
+        values = jnp.concatenate([block(j, 1, lanes) for j in range(9)], axis=0)
+        acc_ref[head] = jnp.dot(
+            lifted.astype(jnp.bfloat16), values, preferred_element_type=jnp.float32
+        )
+        lane = lax.broadcasted_iota(jnp.int32, (ROWS, HEAD_DIM), 1)
+        stat_ref[head] = jnp.where(lane < HEAD_DIM // 2, largest, total)
+
+
 def exchange_kernel(*refs):
-    picked, got, between = refs[:3], refs[3:6], refs[6:9]
-    local_sem, send_sem, mid_sem, last_sem = refs[9:]
+    picked, (kv_ref, q_ref), got, between = refs[:3], refs[3:5], refs[5:8], refs[8:11]
+    acc_ref, stat_ref, window_ref = refs[11:14]
+    local_sem, send_sem, mid_sem, last_sem, halo_send_sem, halo_sem = refs[14:]
     me = position()
+    t, h = lax.axis_index("tm"), lax.axis_index("height")
+    t_count, h_count = lax.axis_size("tm"), lax.axis_size("height")
+    later, earlier = (t, (h + 1) % h_count), (t, (h + h_count - 1) % h_count)
+    after, before = ((t + 1) % t_count, h), ((t + t_count - 1) % t_count, h)
     routes = [("x", "y", "z"), ("y", "z", "x"), ("z", "x", "y")]
-    peers = []
+    peers = [later, earlier, after, before]
     for axis in AXES:
         for d in (1, 2, 3):
             for k in (0, 1):
                 peers.append(device(moved(me, **{axis: d}, k=k)))
     peers.append(device(moved(me, k=1)))
     greet(peers)
+    halo = []
+
+    def neighbour(src, a, b, to):
+        copy = pltpu.make_async_remote_copy(
+            src_ref=src,
+            dst_ref=window_ref.at[a, b],
+            send_sem=halo_send_sem.at[len(halo)],
+            recv_sem=halo_sem.at[len(halo)],
+            device_id=to,
+            device_id_type=MESH,
+        )
+        copy.start()
+        halo.append(copy)
+
+    neighbour(kv_ref, 1, 0, later)
+    neighbour(kv_ref, 1, 2, earlier)
+    neighbour(kv_ref, 0, 1, after)
+    neighbour(kv_ref, 2, 1, before)
     middle = []
     for part in range(3):
         second = routes[part][1]
@@ -285,6 +322,11 @@
             group.append(copy)
         middle.append(group)
     for n, d in enumerate((0, 3, 1, 2)):
+        if n == 1:
+            for came, j in ((0, 0), (1, 2)):
+                halo[came].wait_recv()
+                neighbour(window_ref.at[1, j], 0, j, after)
+                neighbour(window_ref.at[1, j], 2, j, before)
         for part in range(3):
             _, second, third = routes[part]
             came = moved(me, **{second: d})[second]
@@ -309,6 +351,20 @@
                             device_id=device(to),
                             device_id_type=MESH,
                         ).start()
+    for copy in halo[2:]:
+        copy.wait_recv()
+    valid = []
+    for a in (-1, 0, 1):
+        for b in (-1, 0, 1):
+            inside = (t + a >= 0) & (t + a < t_count) & (h + b >= 0) & (h + b < h_count)
+            valid.append(inside.astype(jnp.int32))
+
+    @pl.loop(0, HEADS // PAIR)
+    def _(i):
+        window_heads(i, valid, q_ref, kv_ref, window_ref, acc_ref, stat_ref)
+
+    for copy in halo:
+        copy.wait_send()
     for part in range(3):
         whole = got[part].at[:, :, :, 0:14]
         pltpu.make_async_copy(whole, whole, last_sem.at[part]).wait()
@@ -319,25 +375,31 @@
         pltpu.make_async_copy(some, some, send_sem.at[part, 0]).wait()
 
 
-def exchange(picked):
+def exchange(picked, kv, queries):
     hbm = pl.BlockSpec(memory_space=pl.ANY)
+    vmem = pl.BlockSpec(memory_space=pltpu.VMEM)
     got = [jax.ShapeDtypeStruct((4, 4, 2, 16, r, HEAD_DIM), picked[0].dtype) for r in PART_ROWS]
     between = [jax.ShapeDtypeStruct(p.shape, p.dtype) for p in picked]
+    stat = jax.ShapeDtypeStruct((HEADS, ROWS, HEAD_DIM), jnp.float32)
     outs = pl.pallas_call(
         exchange_kernel,
         name="exchange",
-        out_shape=got + between,
-        in_specs=[hbm] * 3,
-        out_specs=[hbm] * 6,
+        out_shape=got + between + [stat, stat],
+        in_specs=[hbm] * 3 + [vmem] * 2,
+        out_specs=[hbm] * 6 + [vmem] * 2,
         scratch_shapes=[
+            pltpu.VMEM((3, 3) + kv.shape, kv.dtype),
             pltpu.SemaphoreType.DMA((3,)),
             pltpu.SemaphoreType.DMA((3, 2)),
             pltpu.SemaphoreType.DMA((3, 3)),
             pltpu.SemaphoreType.DMA((3,)),
+            pltpu.SemaphoreType.DMA((8,)),
+            pltpu.SemaphoreType.DMA((8,)),
         ],
         compiler_params=pltpu.CompilerParams(collective_id=1, has_side_effects=True),
-    )(*picked)
-    return [g.reshape(SLOTS, r, HEAD_DIM) for g, r in zip(outs[:3], PART_ROWS)]
+    )(*picked, kv, queries)
+    tiles = [g.reshape(SLOTS, r, HEAD_DIM) for g, r in zip(outs[:3], PART_ROWS)]
+    return tiles, outs[6], outs[7]
 
 
 def asked_codes(tables):
@@ -358,66 +420,6 @@
         jnp.transpose(part1, (1, 2, 0, 4, 3)).reshape(SLOTS),
         jnp.transpose(part2, (2, 1, 0, 4, 3)).reshape(SLOTS),
     ]
-
-
-def window_kernel(valid_ref, q_ref, *refs):
-    own_ref, window_ref, acc_ref, stat_ref = refs
-
-    def block(j, kind, lanes):
-        if j == 4:
-            return own_ref[:, kind, :, lanes].reshape(ROWS, HEAD_DIM)
-        return window_ref[j // 3, j % 3, :, kind, :, lanes].reshape(ROWS, HEAD_DIM)
-
-    for p in range(PAIR):
-        lanes = slice(p * HEAD_DIM, (p + 1) * HEAD_DIM)
-        query = q_ref[:, lanes]
-        parts = []
-        for j in range(9):
-            keys = block(j, 0, lanes)
-            score = lax.dot_general(
-                query, keys, (((1,), (1,)), ((), ())), preferred_element_type=jnp.float32
-            )
-            parts.append(jnp.where(valid_ref[j] > 0, score, NEG))
-        scores = jnp.concatenate(parts, axis=-1)
-        largest = jnp.max(scores, axis=-1, keepdims=True)
-        lifted = jnp.exp2((scores - largest) * EXP2_SCALE)
-        total = jnp.sum(lifted, axis=-1, keepdims=True)
-        values = jnp.concatenate(
-            [block(j, 1, lanes) for j in range(9)], axis=0
-        )
-        acc_ref[p] = jnp.dot(
-            lifted.astype(jnp.bfloat16), values, preferred_element_type=jnp.float32
-        )
-        lane = lax.broadcasted_iota(jnp.int32, (ROWS, HEAD_DIM), 1)
-        stat_ref[p] = jnp.where(lane < HEAD_DIM // 2, largest, total)
-
-
-def window_attention(valid, queries, kv, window):
-    steps = HEADS // PAIR
-    width = PAIR * HEAD_DIM
-    stat = jax.ShapeDtypeStruct((HEADS, ROWS, HEAD_DIM), jnp.float32)
-    block = pl.BlockSpec((NW, 2, CUBE, width), lambda i, v: (0, 0, 0, i))
-    out = pl.BlockSpec((PAIR, ROWS, HEAD_DIM), lambda i, v: (i, 0, 0))
-    return pl.pallas_call(
-        window_kernel,
-        name="window_attention",
-        out_shape=(stat, stat),
-        grid_spec=pltpu.PrefetchScalarGridSpec(
-            num_scalar_prefetch=1,
-            grid=(steps,),
-            in_specs=[
-                pl.BlockSpec((ROWS, width), lambda i, v: (0, i)),
-                block,
-                pl.BlockSpec((3, 3, NW, 2, CUBE, width), lambda i, v: (0, 0, 0, 0, 0, i)),
-            ],
-            out_specs=(out, out),
-        ),
-        cost_estimate=pl.CostEstimate(
-            flops=HEADS * 4 * ROWS * 9 * ROWS * HEAD_DIM,
-            bytes_accessed=20_000_000,
-            transcendentals=HEADS * ROWS * 9 * ROWS,
-        ),
-    )(valid, queries, kv, window)
 
 
 def far_kernel(
@@ -507,16 +509,9 @@
     far = far_cubes.reshape(NW, HEADS, FAR)
     requests, far_slot = request_tables(far, device_count)
     kv = keys_values.reshape(NW, 2, CUBE, model)
-    window, *rows, tables = spread(kv, requests)
-    tiles = exchange(pick(asked_codes(tables), rows))
-    offsets = jnp.arange(3, dtype=jnp.int32) - 1
-    times = lax.axis_index("tm") + offsets
-    heights = lax.axis_index("height") + offsets
-    valid = ((times >= 0) & (times < tm_count))[:, None]
-    valid = valid & ((heights >= 0) & (heights < height_count))[None, :]
-    valid = valid.reshape(9).astype(jnp.int32)
+    *rows, tables = spread(kv, requests)
     flat_queries = queries.reshape(ROWS, model)
-    acc, stat = window_attention(valid, flat_queries, kv, window)
+    tiles, acc, stat = exchange(pick(asked_codes(tables), rows), kv, flat_queries)
     output = far_attention(
         far_slot.reshape(NW * HEADS * FAR), flat_queries, tiles, acc, stat, out_weight
     )

time: 323 us -> 278 us (0.86)
  Pallas kernels: 308 us -> 263 us
    pallas_call x3 -> x2, Pallas kernels: 258 us -> 213 us  [the longest x1 181 us: exchange(): pl.pallas_call(exchange_kernel, name='exchange', out_shape=got + between...]
where the time goes in v3:
time: 278 us
  Pallas kernels  263 us (95%)
  local copies, waits for them, and re-layouts  12.2 us (4%)
    pallas_call x1, Pallas kernels, exchange(): pl.pallas_call(exchange_kernel, name='exchange', out_shape=got + between...  181 us
    pallas_call x1, Pallas kernels, far_attention(): pl.pallas_call(far_kernel, name='far_attention', out_shape=jax.ShapeDtype...  35 us
    pallas_call x1, Pallas kernels, spread(): pl.pallas_call(spread_kernel, name='spread', out_shape=(*rows, jax.ShapeD...  31.9 us
    pallas_call x1, Pallas kernels, pick(): pl.pallas_call(pick_kernel, name='pick_tiles', out_shape=[jax.ShapeDtypeS...  15 us
    pallas_call x1, local copies, waits for them, and re-layouts, spread(): pl.pallas_call(spread_kernel, name='spread', out_shape=(*rows, jax.ShapeD...  5.84 us

profile of v3, /device:TPU:1, one launch (start us, length us, event | category | flops | bytes accessed | tf_op | source)
XLA Modules:
  0.0 277.9 jit_solution(9115004701512370848)
XLA Ops:
  0.0 0.8 copy.31
  0.8 0.2 fusion
  1.0 0.1 copy.32
  1.2 0.1 reshape.81
  1.3 0.1 copy.33
  1.3 0.2 broadcast_add_fusion
  1.6 0.7 select_reduce_fusion.1
  2.3 0.1 copy.34
  2.4 0.1 copy.35
  2.5 1.0 select_reduce_fusion
  3.5 0.1 reduce_sum.21
  3.6 0.6 multiply_add_fusion.slot_ref
  4.2 31.9 %spread.1 = (bf16[4,2,48,3072]{3,2,1,0:T(8,128)(2,1)}, bf16[4,2,48,3072]{3,2,1,0:T(8,128)(2,1)}, bf16[4,2,32,3072]{3,2,1,0:T(8,128)(2,1)}, s32[2,4,4,4,8,128]{5,4,3,2,1,0:T(8,128)}) custom-call(bf16[2,2,64,3072]{3,2,1,0:T(8,128)(2,1)} %bitcast.36, s32[8,128]{1,0:T(8,128)} %bitcast.50), custom_call_target="tpu_custom_call" | custom-call | tf_op jit(solution)/shard_map/spread/pallas_call | solution.py:191
  36.1 5.8 %copy.36 = s32[2,4,4,4,8,128]{4,5,3,2,1,0:T(8,128)} copy(s32[2,4,4,4,8,128]{5,4,3,2,1,0:T(8,128)} %get-tuple-element.17) | data formatting | bytes 1048576 | tf_op jit(solution)/shard_map/spread/pallas_call | solution.py:191
  41.9 1.0 constant_dynamic-slice_fusion.1
  43.0 0.7 reshape.89.code2
  43.7 1.0 constant_dynamic-slice_fusion
  44.7 0.9 dynamic-slice_bitcast_fusion
  45.6 0.7 reshape.87.code0
  46.3 0.7 reshape.88.code1
  47.0 15.0 %pick_tiles.1 = (bf16[4,4,32,48,128]{4,3,2,1,0:T(8,128)(2,1)}, bf16[4,4,32,48,128]{4,3,2,1,0:T(8,128)(2,1)}, bf16[4,4,32,32,128]{4,3,2,1,0:T(8,128)(2,1)}) custom-call(s32[512]{0:T(512)} %reshape.87.code0, s32[512]{0:T(512)} %reshape.88.code1, s32[512]{0:T(512)} %reshape.89.code2, bf16[4,2,48,3072]{3,2,1,0:T(8,128)(2,1)} %get-tuple-element.18.rows0, ...), custom_call_target="tpu_custom_call" | custom-call | tf_op jit(solution)/shard_map/pick_tiles/pallas_call | solution.py:226
  62.0 180.9 %exchange.1 = (bf16[4,4,2,16,48,128]{5,4,3,2,1,0:T(8,128)(2,1)}, bf16[4,4,2,16,48,128]{5,4,3,2,1,0:T(8,128)(2,1)}, bf16[4,4,2,16,32,128]{5,4,3,2,1,0:T(8,128)(2,...) custom-call(bf16[4,4,32,48,128]{4,3,2,1,0:T(8,128)(2,1)} %get-tuple-, ...), custom_call_target="tpu_custom_call" | custom-call | tf_op jit(solution)/shard_map/exchange/pallas_call | solution.py:384
  242.9 35.0 %far_attention.1 = bf16[128,3072]{1,0:T(8,128)(2,1)} custom-call(s32[768]{0:T(1024)} %multiply_add_fusion.slot_ref, bf16[128,3072]{1,0:T(8,128)(2,1)} %bitcast.42, bf16[512,48,128]{2,1,0:T(8,128)(2,1)} %bitcast.38, bf16[512,48,128]{2,1,0:T(8,128)(2,1)} %bitcast.39, bf16[512,32,128]{2,1,0:T(8,128)(2,1)} %bitcast.40, ...), custom_call_target="tpu_custom_call" | custom-call | flops 4026531840 | bytes 50000000 | tf_op jit(solution)/shard_map/far_attention/pallas_call | solution.py:476
  (5 shorter events, 0.1 us)

commit v4 on v3

--- a/solution.py
+++ b/solution.py
@@ -32,8 +32,7 @@
     rank = jnp.dot(wanted.astype(jnp.bfloat16), before, preferred_element_type=jnp.float32)
     rank = rank.astype(jnp.int32)
     chosen = wanted[:, :, None] & (rank[:, :, None] == jnp.arange(2 * capacity, dtype=jnp.int32))
-    labels = codes // HEADS * 32 + codes % HEADS
-    requests = jnp.sum(jnp.where(chosen, labels[None, :, None], 0), axis=1)
+    requests = jnp.sum(jnp.where(chosen, codes[None, :, None], 0), axis=1)
     slot = rank + jnp.arange(device_count, dtype=jnp.int32)[:, None] * capacity
     slot = jnp.transpose(slot.reshape(device_count, NW, HEADS), (2, 0, 1)).reshape(HEADS, cubes)
     far_slot = jnp.sum(jnp.where(hit, slot[None, :, None, :], 0), axis=-1)
@@ -207,40 +206,6 @@
     )(kv, table)
 
 
-def pick_kernel(code0, code1, code2, rows0, rows1, rows2, out0, out1, out2):
-    step = pl.program_id(0) * 4 + pl.program_id(1)
-    tiles = 32
-
-    def one(i, carry):
-        for code_ref, rows, out in ((code0, rows0, out0), (code1, rows1, out1), (code2, rows2, out2)):
-            code = code_ref[step * tiles + i]
-            lane = pl.multiple_of((code & 31) * HEAD_DIM, HEAD_DIM)
-            out[0, 0, i] = rows[(i >> 2) & 3, code >> 5, :, pl.ds(lane, HEAD_DIM)]
-        return carry
-
-    lax.fori_loop(0, tiles, one, 0, unroll=8)
-
-
-def pick(codes, rows):
-    shapes = [(4, 4, 32, r, HEAD_DIM) for r in PART_ROWS]
-    return pl.pallas_call(
-        pick_kernel,
-        name="pick_tiles",
-        out_shape=[jax.ShapeDtypeStruct(s, rows[0].dtype) for s in shapes],
-        grid_spec=pltpu.PrefetchScalarGridSpec(
-            num_scalar_prefetch=3,
-            grid=(4, 4),
-            in_specs=[
-                pl.BlockSpec(r.shape, lambda i, j, *c: (0, 0, 0, 0), pipeline_mode=pl.Buffered(1))
-                for r in rows
-            ],
-            out_specs=[
-                pl.BlockSpec((1, 1) + s[2:], lambda i, j, *c: (i, j, 0, 0, 0)) for s in shapes
-            ],
-        ),
-    )(*codes, *rows)
-
-
 def window_heads(i, valid, q_ref, own_ref, window_ref, acc_ref, stat_ref):
     def block(j, kind, lanes):
         ref = own_ref if j == 4 else window_ref.at[j // 3, j % 3]
@@ -270,9 +235,18 @@
 
 
 def exchange_kernel(*refs):
-    picked, (kv_ref, q_ref), got, between = refs[:3], refs[3:5], refs[5:8], refs[8:11]
-    acc_ref, stat_ref, window_ref = refs[11:14]
-    local_sem, send_sem, mid_sem, last_sem, halo_send_sem, halo_sem = refs[14:]
+    code_ref, rows_refs, (kv_ref, q_ref) = refs[0], refs[1:4], refs[4:6]
+    got, between, picked, (acc_ref, stat_ref) = refs[6:9], refs[9:12], refs[12:15], refs[15:17]
+    window_ref, rows, chosen = refs[17], refs[18:21], refs[21:24]
+    local_sem, send_sem, mid_sem, last_sem, halo_send_sem, halo_sem, rows_sem, chosen_sem = refs[24:]
+    for part in range(3):
+        for code in range(NW * HEADS):
+            lane = code % HEADS * HEAD_DIM
+            pltpu.make_async_copy(
+                rows_refs[part].at[:, code // HEADS, :, lane : lane + HEAD_DIM],
+                rows[part].at[:, code],
+                rows_sem.at[part],
+            ).start()
     me = position()
     t, h = lax.axis_index("tm"), lax.axis_index("height")
     t_count, h_count = lax.axis_size("tm"), lax.axis_size("height")
@@ -304,23 +278,55 @@
     neighbour(kv_ref, 1, 2, earlier)
     neighbour(kv_ref, 0, 1, after)
     neighbour(kv_ref, 2, 1, before)
-    middle = []
     for part in range(3):
+        pltpu.make_async_copy(rows[part], rows[part], rows_sem.at[part]).wait()
+
+    def pick(part, group):
+        first, second, third = routes[part]
+
+        @pl.loop(0, 4)
+        def _(j):
+            asker = {first: me[first], second: group, third: j}
+            at = ((asker["z"] * 4 + asker["y"]) * 4 + asker["x"]) * 8
+            for k in range(2):
+                for holder in range(4):
+                    for slot in range(4):
+                        code = code_ref[part * 4 + holder, at + k * 512 + slot]
+                        chosen[part][group, j, (k * 4 + holder) * 4 + slot] = rows[part][holder, code]
+
+    middle = [[], [], []]
+
+    def pass_on(part, n, d, copy):
+        copy.wait()
+        if d == 0:
+            return
         second = routes[part][1]
-        group = []
-        for n, d in enumerate((1, 3, 2)):
-            to = moved(me, **{second: d})
-            copy = pltpu.make_async_remote_copy(
-                src_ref=picked[part].at[to[second]],
-                dst_ref=between[part].at[me[second]],
-                send_sem=send_sem.at[part, 0],
-                recv_sem=mid_sem.at[part, n],
-                device_id=device(to),
-                device_id_type=MESH,
+        to = moved(me, **{second: d})
+        sending = pltpu.make_async_remote_copy(
+            src_ref=picked[part].at[to[second]],
+            dst_ref=between[part].at[me[second]],
+            send_sem=send_sem.at[part, 0],
+            recv_sem=mid_sem.at[part, n],
+            device_id=device(to),
+            device_id_type=MESH,
+        )
+        sending.start()
+        middle[part].append(sending)
+
+    waiting = None
+    for n, d in enumerate((1, 3, 2, 0)):
+        for part in range(3):
+            second = routes[part][1]
+            group = moved(me, **{second: d})[second]
+            pick(part, group)
+            copy = pltpu.make_async_copy(
+                chosen[part].at[group], picked[part].at[group], chosen_sem.at[part, n]
             )
             copy.start()
-            group.append(copy)
-        middle.append(group)
+            if waiting is not None:
+                pass_on(*waiting)
+            waiting = (part, n, d, copy)
+    pass_on(*waiting)
     for n, d in enumerate((0, 3, 1, 2)):
         if n == 1:
             for came, j in ((0, 0), (1, 2)):
@@ -375,51 +381,59 @@
         pltpu.make_async_copy(some, some, send_sem.at[part, 0]).wait()
 
 
-def exchange(picked, kv, queries):
+def exchange(codes, rows, kv, queries):
     hbm = pl.BlockSpec(memory_space=pl.ANY)
     vmem = pl.BlockSpec(memory_space=pltpu.VMEM)
-    got = [jax.ShapeDtypeStruct((4, 4, 2, 16, r, HEAD_DIM), picked[0].dtype) for r in PART_ROWS]
-    between = [jax.ShapeDtypeStruct(p.shape, p.dtype) for p in picked]
+    smem = pl.BlockSpec(memory_space=pltpu.SMEM)
+    got = [jax.ShapeDtypeStruct((4, 4, 2, 16, r, HEAD_DIM), kv.dtype) for r in PART_ROWS]
+    picked = [jax.ShapeDtypeStruct((4, 4, 32, r, HEAD_DIM), kv.dtype) for r in PART_ROWS]
     stat = jax.ShapeDtypeStruct((HEADS, ROWS, HEAD_DIM), jnp.float32)
     outs = pl.pallas_call(
         exchange_kernel,
         name="exchange",
-        out_shape=got + between + [stat, stat],
-        in_specs=[hbm] * 3 + [vmem] * 2,
-        out_specs=[hbm] * 6 + [vmem] * 2,
+        out_shape=got + picked + picked + [stat, stat],
+        in_specs=[smem] + [hbm] * 3 + [vmem] * 2,
+        out_specs=[hbm] * 9 + [vmem] * 2,
         scratch_shapes=[
             pltpu.VMEM((3, 3) + kv.shape, kv.dtype),
+            *[pltpu.VMEM((4, NW * HEADS, r, HEAD_DIM), kv.dtype) for r in PART_ROWS],
+            *[pltpu.VMEM(p.shape, p.dtype) for p in picked],
             pltpu.SemaphoreType.DMA((3,)),
             pltpu.SemaphoreType.DMA((3, 2)),
             pltpu.SemaphoreType.DMA((3, 3)),
             pltpu.SemaphoreType.DMA((3,)),
             pltpu.SemaphoreType.DMA((8,)),
             pltpu.SemaphoreType.DMA((8,)),
+            pltpu.SemaphoreType.DMA((3,)),
+            pltpu.SemaphoreType.DMA((3, 4)),
         ],
-        compiler_params=pltpu.CompilerParams(collective_id=1, has_side_effects=True),
-    )(*picked, kv, queries)
+        compiler_params=pltpu.CompilerParams(
+            collective_id=1, has_side_effects=True, vmem_limit_bytes=60 * 1024 * 1024
+        ),
+    )(codes, *rows, kv, queries)
     tiles = [g.reshape(SLOTS, r, HEAD_DIM) for g, r in zip(outs[:3], PART_ROWS)]
-    return tiles, outs[6], outs[7]
+    return tiles, outs[9], outs[10]
 
 
 def asked_codes(tables):
     at = position()
-    t = tables.reshape(2, 4, 4, 4, 8, 4, 2, 4, 4)[:, :, :, :, :4]
-    t = lax.dynamic_index_in_dim(t, at["k"], 6, keepdims=False)
-
-    def take(value, which):
-        for axis, name in which:
-            value = lax.dynamic_index_in_dim(value, at[name], axis, keepdims=True)
-        return value
-
-    part0 = take(t, ((3, "x"), (5, "y"), (6, "z")))[:, :, :, 0, :, 0, 0, :]
-    part1 = take(t, ((2, "y"), (6, "z"), (7, "x")))[:, :, 0, :, :, :, 0, 0]
-    part2 = take(t, ((1, "z"), (5, "y"), (7, "x")))[:, 0, :, :, :, 0, :, 0]
-    return [
-        jnp.transpose(part0, (2, 1, 0, 4, 3)).reshape(SLOTS),
-        jnp.transpose(part1, (1, 2, 0, 4, 3)).reshape(SLOTS),
-        jnp.transpose(part2, (2, 1, 0, 4, 3)).reshape(SLOTS),
-    ]
+    holder = jnp.arange(4, dtype=jnp.int32)
+    column = at["y"] * 32 + at["k"] * 16 + at["z"] * 4 + at["x"]
+    columns = jnp.concatenate(
+        [
+            column + (holder - at["x"]),
+            column + (holder - at["y"]) * 32,
+            column + (holder - at["z"]) * 4,
+        ]
+    )
+    mine = columns[:, None] == jnp.arange(tables.shape[-1], dtype=jnp.int32)
+    asked = lax.dot_general(
+        mine.astype(jnp.bfloat16),
+        tables.reshape(-1, tables.shape[-1]).astype(jnp.bfloat16),
+        (((1,), (1,)), ((), ())),
+        preferred_element_type=jnp.float32,
+    )
+    return asked.astype(jnp.int32)
 
 
 def far_kernel(
@@ -511,7 +525,7 @@
     kv = keys_values.reshape(NW, 2, CUBE, model)
     *rows, tables = spread(kv, requests)
     flat_queries = queries.reshape(ROWS, model)
-    tiles, acc, stat = exchange(pick(asked_codes(tables), rows), kv, flat_queries)
+    tiles, acc, stat = exchange(asked_codes(tables), rows, kv, flat_queries)
     output = far_attention(
         far_slot.reshape(NW * HEADS * FAR), flat_queries, tiles, acc, stat, out_weight
     )

time: 278 us -> 256 us (0.921)
  Pallas kernels: 263 us -> 249 us
  local copies, waits for them, and re-layouts: 12.2 us -> 1.33 us
    pallas_call x2 -> x1, Pallas kernels: 196 us -> 182 us  [exchange(): pl.pallas_call(exchange_kernel, name='exchange', out_shape=got + picked +...]
    pallas_call x1 -> x0, local copies, waits for them, and re-layouts: 5.84 us -> none  [spread(): pl.pallas_call(spread_kernel, name='spread', out_shape=(*rows, jax.ShapeD...]
where the time goes in v4:
time: 256 us
  Pallas kernels  249 us (97%)
  other arithmetic  3.71 us (1%)
    pallas_call x1, Pallas kernels, exchange(): pl.pallas_call(exchange_kernel, name='exchange', out_shape=got + picked +...  182 us
    pallas_call x1, Pallas kernels, far_attention(): pl.pallas_call(far_kernel, name='far_attention', out_shape=jax.ShapeDtype...  35 us
    pallas_call x1, Pallas kernels, spread(): pl.pallas_call(spread_kernel, name='spread', out_shape=(*rows, jax.ShapeD...  31.9 us

profile of v4, /device:TPU:1, one launch (start us, length us, event | category | flops | bytes accessed | tf_op | source)
XLA Modules:
  0.0 255.5 jit_solution(8301771514032498396)
XLA Ops:
  0.0 0.1 pad_add_fusion
  0.1 0.8 copy.13
  0.9 0.2 fusion
  1.1 0.1 copy.14
  1.3 0.1 reshape.41
  1.3 0.1 copy.15
  1.4 0.2 broadcast_add_fusion
  1.6 0.6 select_reduce_fusion.1
  2.3 0.1 copy.16
  2.4 0.1 copy.17
  2.5 1.0 select_reduce_fusion
  3.5 0.1 reduce_sum.21
  3.6 0.6 multiply_add_fusion.slot_ref
  4.2 31.9 %spread.1 = (bf16[4,2,48,3072]{3,2,1,0:T(8,128)(2,1)}, bf16[4,2,48,3072]{3,2,1,0:T(8,128)(2,1)}, bf16[4,2,32,3072]{3,2,1,0:T(8,128)(2,1)}, s32[2,4,4,4,8,128]{5,4,3,2,1,0:T(8,128)}) custom-call(bf16[2,2,64,3072]{3,2,1,0:T(8,128)(2,1)} %bitcast.19, s32[8,128]{1,0:T(8,128)} %bitcast.32), custom_call_target="tpu_custom_call" | custom-call | tf_op jit(solution)/shard_map/spread/pallas_call | solution.py:190
  36.1 1.1 convert_element_type.16
  37.2 0.9 convolution_convert_fusion.refs_0_
  38.0 182.5 %exchange.1 = (bf16[4,4,2,16,48,128]{5,4,3,2,1,0:T(8,128)(2,1)}, bf16[4,4,2,16,48,128]{5,4,3,2,1,0:T(8,128)(2,1)}, bf16[4,4,2,16,32,128]{5,4,3,2,1,0:T(8,128)(2,...) custom-call(s32[12,1024]{1,0:T(8,128)} %convolution_convert_fusion.r, ...), custom_call_target="tpu_custom_call" | custom-call | tf_op jit(solution)/shard_map/exchange/pallas_call | solution.py:391
  220.5 35.0 %far_attention.1 = bf16[128,3072]{1,0:T(8,128)(2,1)} custom-call(s32[768]{0:T(1024)} %multiply_add_fusion.slot_ref, bf16[128,3072]{1,0:T(8,128)(2,1)} %bitcast.25, bf16[512,48,128]{2,1,0:T(8,128)(2,1)} %bitcast.21, bf16[512,48,128]{2,1,0:T(8,128)(2,1)} %bitcast.22, bf16[512,32,128]{2,1,0:T(8,128)(2,1)} %bitcast.23, ...), custom_call_target="tpu_custom_call" | custom-call | flops 4026531840 | bytes 50000000 | tf_op jit(solution)/shard_map/far_attention/pallas_call | solution.py:490
  (3 shorter events, 0.0 us)

commit v5 on v4

--- a/solution.py
+++ b/solution.py
@@ -15,6 +15,7 @@
 NW = 2
 SLOTS = 512
 PAIR = 2
+GROUP = 4
 ROWS = NW * CUBE
 NEG = -1e30
 EXP2_SCALE = math.log2(math.e) / math.sqrt(HEAD_DIM)
@@ -44,11 +45,11 @@
     return requests.T, in_x + in_y * SLOTS + in_z * SLOTS * SLOTS
 
 
-PART_ROWS = (48, 48, 32)
+PART_ROWS = (48, 64, 16)
 PIECES = (
     ((0, 0, 48, 0),),
-    ((0, 48, 64, 0), (1, 0, 32, 16)),
-    ((1, 32, 64, 0),),
+    ((0, 48, 64, 0), (1, 0, 48, 16)),
+    ((1, 48, 64, 0),),
 )
 AXES = ("x", "y", "z")
 MESH = pl.DeviceIdType.MESH
@@ -447,17 +448,17 @@
         total[...] = jnp.zeros_like(total)
 
     heads = []
-    for p in range(PAIR):
+    for p in range(GROUP):
         cubes = []
         for c in range(NW):
             rows = slice(c * CUBE, (c + 1) * CUBE)
             query = q_ref[rows, p * HEAD_DIM : (p + 1) * HEAD_DIM]
             keys, values = [], []
             for f in range(FAR):
-                slot = slot_ref[(c * HEADS + step * PAIR + p) * FAR + f]
+                slot = slot_ref[(c * HEADS + step * GROUP + p) * FAR + f]
                 in0, in1, in2 = slot & (SLOTS - 1), (slot >> 9) & (SLOTS - 1), slot >> 18
                 keys += [tiles0[in0], tiles1[in1, 0:16]]
-                values += [tiles1[in1, 16:48], tiles2[in2]]
+                values += [tiles1[in1, 16:64], tiles2[in2]]
             keys = jnp.concatenate(keys, axis=0)
             values = jnp.concatenate(values, axis=0)
             scores = lax.dot_general(
@@ -483,10 +484,10 @@
 
 
 def far_attention(far_slot, queries, tiles, acc, stat, out_weight):
-    steps = HEADS // PAIR
-    width = PAIR * HEAD_DIM
+    steps = HEADS // GROUP
+    width = GROUP * HEAD_DIM
     model = queries.shape[1]
-    near = pl.BlockSpec((PAIR, ROWS, HEAD_DIM), lambda i, s: (i, 0, 0))
+    near = pl.BlockSpec((GROUP, ROWS, HEAD_DIM), lambda i, s: (i, 0, 0))
     return pl.pallas_call(
         far_kernel,
         name="far_attention",

time: 256 us -> 284 us (1.11)
  Pallas kernels: 249 us -> 277 us
    pallas_call x1, Pallas kernels: 182 us -> 205 us  [exchange(): pl.pallas_call(exchange_kernel, name='exchange', out_shape=got + picked +...]
    pallas_call x1, Pallas kernels: 31.9 us -> 38.2 us  [spread(): pl.pallas_call(spread_kernel, name='spread', out_shape=(*rows, jax.ShapeD...]
where the time goes in v5:
time: 284 us; the launch traced here: 283 us
  Pallas kernels  277 us (98%)
  other arithmetic  3.71 us (1%)
    pallas_call x1, Pallas kernels, exchange(): pl.pallas_call(exchange_kernel, name='exchange', out_shape=got + picked +...  205 us
    pallas_call x1, Pallas kernels, spread(): pl.pallas_call(spread_kernel, name='spread', out_shape=(*rows, jax.ShapeD...  38.2 us
    pallas_call x1, Pallas kernels, far_attention(): pl.pallas_call(far_kernel, name='far_attention', out_shape=jax.ShapeDtype...  33.8 us

profile of v5, /device:TPU:1, one launch (start us, length us, event | category | flops | bytes accessed | tf_op | source)
XLA Modules:
  0.0 283.3 jit_solution(5688492932195512260)
XLA Ops:
  0.0 0.1 pad_add_fusion
  0.1 0.8 copy.13
  0.9 0.2 fusion
  1.1 0.1 copy.14
  1.3 0.1 reshape.41
  1.3 0.1 copy.15
  1.4 0.2 broadcast_add_fusion
  1.6 0.6 select_reduce_fusion.1
  2.3 0.1 copy.16
  2.4 0.1 copy.17
  2.5 1.0 select_reduce_fusion
  3.5 0.1 reduce_sum.21
  3.6 0.6 multiply_add_fusion.slot_ref
  4.2 38.2 %spread.1 = (bf16[4,2,48,3072]{3,2,1,0:T(8,128)(2,1)}, bf16[4,2,64,3072]{3,2,1,0:T(8,128)(2,1)}, bf16[4,2,16,3072]{3,2,1,0:T(8,128)(2,1)}, s32[2,4,4,4,8,128]{5,4,3,2,1,0:T(8,128)}) custom-call(bf16[2,2,64,3072]{3,2,1,0:T(8,128)(2,1)} %bitcast.20, s32[8,128]{1,0:T(8,128)} %bitcast.32), custom_call_target="tpu_custom_call" | custom-call | tf_op jit(solution)/shard_map/spread/pallas_call | solution.py:191
  42.4 1.1 convert_element_type.16
  43.5 0.9 convolution_convert_fusion.refs_0_
  44.4 205.1 %exchange.1 = (bf16[4,4,2,16,48,128]{5,4,3,2,1,0:T(8,128)(2,1)}, bf16[4,4,2,16,64,128]{5,4,3,2,1,0:T(8,128)(2,1)}, bf16[4,4,2,16,16,128]{5,4,3,2,1,0:T(8,128)(2,...) custom-call(s32[12,1024]{1,0:T(8,128)} %convolution_convert_fusion.r, ...), custom_call_target="tpu_custom_call" | custom-call | tf_op jit(solution)/shard_map/exchange/pallas_call | solution.py:392
  249.5 33.8 %far_attention.1 = bf16[128,3072]{1,0:T(8,128)(2,1)} custom-call(s32[768]{0:T(1024)} %multiply_add_fusion.slot_ref, bf16[128,3072]{1,0:T(8,128)(2,1)} %bitcast.24, bf16[512,48,128]{2,1,0:T(8,128)(2,1)} %bitcast.22, bf16[512,64,128]{2,1,0:T(8,128)(2,1)} %bitcast.19, bf16[512,16,128]{2,1,0:T(8,128)(2,1)} %bitcast.25, ...), custom_call_target="tpu_custom_call" | custom-call | flops 4026531840 | bytes 50000000 | tf_op jit(solution)/shard_map/far_attention/pallas_call | solution.py:491
  (3 shorter events, 0.0 us)

commit v6 on v5

--- a/solution.py
+++ b/solution.py
@@ -45,11 +45,11 @@
     return requests.T, in_x + in_y * SLOTS + in_z * SLOTS * SLOTS
 
 
-PART_ROWS = (48, 64, 16)
+PART_ROWS = (48, 48, 32)
 PIECES = (
     ((0, 0, 48, 0),),
-    ((0, 48, 64, 0), (1, 0, 48, 16)),
-    ((1, 48, 64, 0),),
+    ((0, 48, 64, 0), (1, 0, 32, 16)),
+    ((1, 32, 64, 0),),
 )
 AXES = ("x", "y", "z")
 MESH = pl.DeviceIdType.MESH
@@ -334,7 +334,7 @@
                 halo[came].wait_recv()
                 neighbour(window_ref.at[1, j], 0, j, after)
                 neighbour(window_ref.at[1, j], 2, j, before)
-        for part in range(3):
+        for part in (1, 2, 0):
             _, second, third = routes[part]
             came = moved(me, **{second: d})[second]
             if n > 0:
@@ -458,7 +458,7 @@
                 slot = slot_ref[(c * HEADS + step * GROUP + p) * FAR + f]
                 in0, in1, in2 = slot & (SLOTS - 1), (slot >> 9) & (SLOTS - 1), slot >> 18
                 keys += [tiles0[in0], tiles1[in1, 0:16]]
-                values += [tiles1[in1, 16:64], tiles2[in2]]
+                values += [tiles1[in1, 16:48], tiles2[in2]]
             keys = jnp.concatenate(keys, axis=0)
             values = jnp.concatenate(values, axis=0)
             scores = lax.dot_general(

time: 284 us -> 255 us (0.90)
  Pallas kernels: 277 us -> 248 us
    pallas_call x1, Pallas kernels: 205 us -> 182 us  [exchange(): pl.pallas_call(exchange_kernel, name='exchange', out_shape=got + picked +...]
    pallas_call x1, Pallas kernels: 38.2 us -> 31.9 us  [spread(): pl.pallas_call(spread_kernel, name='spread', out_shape=(*rows, jax.ShapeD...]
where the time goes in v6:
time: 255 us; the launch traced here: 254 us
  Pallas kernels  248 us (97%)
  other arithmetic  3.71 us (1%)
    pallas_call x1, Pallas kernels, exchange(): pl.pallas_call(exchange_kernel, name='exchange', out_shape=got + picked +...  182 us
    pallas_call x1, Pallas kernels, far_attention(): pl.pallas_call(far_kernel, name='far_attention', out_shape=jax.ShapeDtype...  33.9 us
    pallas_call x1, Pallas kernels, spread(): pl.pallas_call(spread_kernel, name='spread', out_shape=(*rows, jax.ShapeD...  31.9 us

profile of v6, /device:TPU:1, one launch (start us, length us, event | category | flops | bytes accessed | tf_op | source)
XLA Modules:
  0.0 254.5 jit_solution(11917875433779269671)
XLA Ops:
  0.0 0.1 pad_add_fusion
  0.1 0.8 copy.13
  0.9 0.2 fusion
  1.1 0.1 copy.14
  1.3 0.1 reshape.41
  1.3 0.1 copy.15
  1.4 0.2 broadcast_add_fusion
  1.6 0.6 select_reduce_fusion.1
  2.3 0.1 copy.16
  2.4 0.1 copy.17
  2.5 1.0 select_reduce_fusion
  3.5 0.1 reduce_sum.21
  3.6 0.6 multiply_add_fusion.slot_ref
  4.2 31.9 %spread.1 = (bf16[4,2,48,3072]{3,2,1,0:T(8,128)(2,1)}, bf16[4,2,48,3072]{3,2,1,0:T(8,128)(2,1)}, bf16[4,2,32,3072]{3,2,1,0:T(8,128)(2,1)}, s32[2,4,4,4,8,128]{5,4,3,2,1,0:T(8,128)}) custom-call(bf16[2,2,64,3072]{3,2,1,0:T(8,128)(2,1)} %bitcast.19, s32[8,128]{1,0:T(8,128)} %bitcast.32), custom_call_target="tpu_custom_call" | custom-call | tf_op jit(solution)/shard_map/spread/pallas_call | solution.py:191
  36.1 1.1 convert_element_type.16
  37.2 0.9 convolution_convert_fusion.refs_0_
  38.0 182.5 %exchange.1 = (bf16[4,4,2,16,48,128]{5,4,3,2,1,0:T(8,128)(2,1)}, bf16[4,4,2,16,48,128]{5,4,3,2,1,0:T(8,128)(2,1)}, bf16[4,4,2,16,32,128]{5,4,3,2,1,0:T(8,128)(2,...) custom-call(s32[12,1024]{1,0:T(8,128)} %convolution_convert_fusion.r, ...), custom_call_target="tpu_custom_call" | custom-call | tf_op jit(solution)/shard_map/exchange/pallas_call | solution.py:392
  220.5 33.9 %far_attention.1 = bf16[128,3072]{1,0:T(8,128)(2,1)} custom-call(s32[768]{0:T(1024)} %multiply_add_fusion.slot_ref, bf16[128,3072]{1,0:T(8,128)(2,1)} %bitcast.25, bf16[512,48,128]{2,1,0:T(8,128)(2,1)} %bitcast.21, bf16[512,48,128]{2,1,0:T(8,128)(2,1)} %bitcast.22, bf16[512,32,128]{2,1,0:T(8,128)(2,1)} %bitcast.23, ...), custom_call_target="tpu_custom_call" | custom-call | flops 4026531840 | bytes 50000000 | tf_op jit(solution)/shard_map/far_attention/pallas_call | solution.py:491
  (3 shorter events, 0.0 us)
